TPU v7x, 256 devices: a whole 4x4x8 slice. The times are simulated.
256 devices in a mesh: seq: 128 (over z, y, x), chan: 2 (over core).
Axes of the slice: x: 4, y: 4, z: 8, core: 2. Of those that a mesh axis runs over, the one named last changes fastest.
Arguments:
- q_proj: bfloat16 [16384, 8192], P('seq', 'chan'), may hold values from -6 to 6
- k_proj: bfloat16 [16384, 8192], P('seq', 'chan'), may hold values from -6 to 6
- v_proj: bfloat16 [16384, 8192], P('seq', 'chan'), may hold values from -6 to 6
- resid: bfloat16 [16384, 8192], P('seq', 'chan'), may hold values from -6 to 6
- short_filter: float32 [3, 7, 8192], P(None, None, 'chan'), may hold values from -2 to 2
- residue: float32 [8, 8192], P(None, 'chan'), may hold values from -1.5 to 1.5
- rate: float32 [8, 8192], P(None, 'chan'), may hold values from 3.0517578e-05 to 0.0333333333, as said below
- gain: float32 [8192], P('chan'), may hold values from 0.1 to 1.9
- seg_lengths: int32 [16], replicated, may hold values from 1 to 8192, 16384 in all
Outputs:
- stream: bfloat16 [16384, 8192], P('seq', 'chan')
- normed: bfloat16 [16384, 8192], P('seq', 'chan')
Inputs may be any that keep to these rules, and one draw needn't show every extreme that they name: `rate`: rates of the long filter's modes per token, between 0.5 / 16384 and 1 / 30. `seg_lengths`: the lengths sum to 16384.
All inputs are finite; a program needn't handle non-finite values.
Results may differ from a plain program's by a relative error of at most 0.0049.
Values may be sent and summed in bfloat16 or wider, within the bound.
A program may use at most 128 MiB of HBM per device.

v0:
```python
import jax
import jax.numpy as jnp
from jax import lax
from jax.sharding import PartitionSpec as P


def from_behind(shard, axis, by):
    peers = lax.axis_size(axis)
    pairs = [(i, i + by) for i in range(peers) if 0 <= i + by < peers]
    return lax.ppermute(shard, axis, pairs)


def carried_in(value, axis, join, neutral):
    count, mine = (lax.axis_size(axis), lax.axis_index(axis))
    pieces = jax.tree.map(lambda part: lax.all_gather(part, axis), value)
    running = jax.tree.map(
        lambda part, zero: jnp.full_like(part, 0) + jnp.asarray(zero, part.dtype), value, neutral
    )

    def turn(position, running):
        longer = join(running, jax.tree.map(lambda part: part[position], pieces))
        return jax.tree.map(lambda new, old: jnp.where(position < mine, new, old), longer, running)

    return lax.fori_loop(0, count - 1, turn, running)


def local_conv(rim, x, taps):
    width = taps.shape[0]
    count = x.shape[0]
    extended = jnp.concatenate([rim, x], axis=0).astype(jnp.float32)
    out = jnp.zeros(x.shape, jnp.float32)
    for j in range(width):
        out = out + taps[j] * extended[width - 1 - j : width - 1 - j + count]
    return out


def body(q_proj, k_proj, v_proj, resid, short_filter, residue, rate, gain, seg_lengths):
    tok = q_proj.shape[0]
    width = q_proj.shape[1]
    taps = short_filter.shape[1]
    modes = rate.shape[0]
    group = 4
    shard = lax.axis_index("seq")
    rim_q, rim_k, rim_v = from_behind(
        (q_proj[tok - taps + 1 :], k_proj[tok - taps + 1 :], v_proj[tok - taps + 1 :]), "seq", 1
    )
    q_conv = local_conv(rim_q, q_proj, short_filter[0])
    k_conv = local_conv(rim_k, k_proj, short_filter[1])
    v_conv = local_conv(rim_v, v_proj, short_filter[2])
    z_prod = k_conv * v_conv
    ends = jnp.cumsum(seg_lengths)
    local = jnp.arange(tok, dtype=jnp.int32)
    first = shard * tok
    position = first + local
    seg_here = jnp.sum((position[:, None] >= ends[None, :]).astype(jnp.int32), axis=1)
    seg_prev = jnp.sum((first - 1 >= ends).astype(jnp.int32))
    within = ((seg_here[:, None] == seg_here[None, :]) & (local[:, None] >= local[None, :])).astype(
        jnp.float32
    )
    carry_in = (seg_here == seg_prev).astype(jnp.float32)
    through = carry_in[tok - 1]
    centre = (local - tok // 2).astype(jnp.float32)
    step_up = (local + 1).astype(jnp.float32)
    coef = residue * jnp.sqrt(-jnp.expm1(-2.0 * rate))
    intra = jnp.zeros(z_prod.shape, jnp.float32)
    pieces = []
    for lower in range(0, modes, group):
        block_part_rate = rate[lower : lower + group]
        rise = jnp.exp(block_part_rate[:, None, :] * centre[None, :, None])
        summed = jnp.einsum(
            "ts,gsc->gtc", within, rise * z_prod[None], precision=lax.Precision.HIGHEST
        )
        fall = jnp.exp(-block_part_rate[:, None, :] * centre[None, :, None])
        contrib = jnp.sum(coef[lower : lower + group][:, None, :] * fall * summed, axis=0)
        contrib, last_rows = (contrib, fall[:, tok - 1, :] * summed[:, tok - 1, :])
        intra = intra + contrib
        pieces.append(last_rows)
    end_state = jnp.concatenate(pieces, axis=0)
    span = jnp.exp(-rate * tok) * through

    def join_pair(earlier, later):
        return (earlier[0] * later[0], later[0] * earlier[1] + later[1])

    _, incoming = carried_in(
        (span, end_state), "seq", join_pair, (jnp.ones_like(span), jnp.zeros_like(end_state))
    )
    carried = jnp.zeros(z_prod.shape, jnp.float32)
    for lower in range(0, modes, group):
        part_rate = rate[lower : lower + group]
        weights = jnp.exp(-part_rate[:, None, :] * step_up[None, :, None])
        carried = carried + jnp.sum(
            coef[lower : lower + group][:, None, :]
            * weights
            * incoming[lower : lower + group][:, None, :],
            axis=0,
        )
    conv = intra + carried * carry_in[:, None]
    stream = (resid.astype(jnp.float32) + q_conv * conv).astype(jnp.bfloat16)
    widened = stream.astype(jnp.float32)
    square_sum = lax.psum(jnp.sum(widened * widened, axis=1), "chan")
    square_mean = square_sum / (width * lax.axis_size("chan"))
    normed = (widened * lax.rsqrt(square_mean[:, None] + 1e-06) * gain).astype(jnp.bfloat16)
    return (stream, normed)


def solution(mesh):
    placed = (
        P("seq", "chan"),
        P("seq", "chan"),
        P("seq", "chan"),
        P("seq", "chan"),
        P(None, None, "chan"),
        P(None, "chan"),
        P(None, "chan"),
        P("chan"),
        P(),
    )
    return jax.shard_map(
        body,
        mesh=mesh,
        in_specs=placed,
        out_specs=(P("seq", "chan"), P("seq", "chan")),
        check_vma=False,
    )
```

profile of v0, /device:TPU:1, one launch (start us, length us, event | category | flops | bytes accessed | tf_op | source)
XLA Modules:
  0.0 515.2 jit_solution(6396637612879641983)
XLA Ops:
  10.2 2.4 exponential_multiply_fusion.2
  13.5 3.9 collective-permute-start.1
  18.3 3.1 collective-permute-start.2
  22.5 1.1 slice_negate_fusion
  23.6 3.2 fusion.45
  27.4 3.5 fusion.13
  30.9 11.0 %multiply_exponential_fusion.1 = (f32[4,128,4096]{2,0,1:T(4,128)S(1)}, f32[4,128,4096]{2,0,1:T(4,128)}, f32[4,128,4096]{2,0,1:T(4,128)}, f32[4,128,4096]{2,0,1:T(4,128)S(1)}) fusion(f32[128]{0:T(128)S(1)} %add_convert_fusion.1, f32[4,4096]{1,0:T(4,128)S(1)} %get-tuple-element.161, f32[4,4096]{1,0:T(4,128)S(1)} %get-tuple-element.160, ...), kind=kLoop, calls=%fused_computation.16 | loop fusion | flops 12582912 | bytes 35914240 | tf_op jit(solution)/shard_map/exp | solution.py:73
  41.9 11.0 %fusion.1 = f32[4,4096,128]{1,2,0:T(8,128)} fusion(f32[4,128,4096]{2,0,1:T(4,128)S(1)} %get-tuple-element.169, s32[128]{0:T(128)S(1)} %convert_reduce_fusion), kind=kOutput, calls=%fused_computation.4 | convolution fusion | flops 3221274624 | bytes 16777728 | tf_op jit(solution)/shard_map/ts,gsc->gtc/dot_general | solution.py:70
  52.9 12.0 %copy.44 = f32[4,4096,128]{1,0,2:T(4,128)} copy(f32[4,4096,128]{1,2,0:T(8,128)} %fusion.1) | data formatting | bytes 16777216 | tf_op jit(solution)/shard_map/ts,gsc->gtc/dot_general | solution.py:70
  64.9 13.6 %fusion.6 = f32[4,128,4096]{2,1,0:T(8,128)S(1)} fusion(f32[4,128,4096]{2,0,1:T(4,128)} %get-tuple-element.168, s32[128]{0:T(128)S(1)} %convert_reduce_fusion), kind=kOutput, calls=%fused_computation.17 | convolution fusion | flops 3221274624 | bytes 16777728 | tf_op jit(solution)/shard_map/ts,gsc->gtc/dot_general | solution.py:70
  78.6 3.2 copy-done
  83.6 3.4 collective-permute-start
  88.3 1.1 maximum_convert_fusion
  89.4 77.3 %all-gather.5.cloned.1.call-done = f32[1024,4096]{1,0:T(8,128)} async-done(((f32[8,4096]{1,0:T(8,128)}), f32[1024,4096]{1,0:T(8,128)}) %all-gather.5.cloned.1.call-update) | async-done | bytes 16777232 | tf_op jit(solution)/shard_map/all_gather | solution.py:15
  166.7 152.0 %all-gather.7.cloned.1.call-done = f32[1024,4096]{1,0:T(8,128)} async-done(((f32[8,4096]{1,0:T(8,128)}), f32[1024,4096]{1,0:T(8,128)}) %all-gather.7.cloned.1.call-update) | async-done | bytes 16777232 | tf_op jit(solution)/shard_map/all_gather | solution.py:15
  318.8 138.5 %while.14 = (s32[]{:T(128)}, f32[8,4096]{1,0:T(8,128)S(1)}, s32[]{:T(128)}, f32[128,8,4096]{2,1,0:T(8,128)}, f32[128,8,4096]{2,1,0:T(8,128)}, /*index=5*/s32[]{:T(128)}, s32[]{:T(128)}) while((s32[]{:T(128)}, f32[8,4096]{1,0:T(8,128)S(1)}, s32[]{:T(128)}, f32[128,8,4096]{2,1,0:T(8,128)}, f32[128,8,4096]{2,1,0:T(8,128)}, ...), condition=%wide.region_6.7_spmd.clone, body=%wide.region_5.6_spmd.clone.sunk | while | flops 131076 | bytes 524389 | solution.py:24
  321.0 1.1 fusion.50
  323.1 1.1 fusion.50
  326.4 1.1 fusion.50
  329.7 1.1 fusion.50
  331.9 1.1 fusion.50
  335.1 1.1 fusion.50
  338.4 1.1 fusion.50
  341.7 1.1 fusion.50
  343.9 1.1 fusion.50
  347.1 1.1 fusion.50
  350.4 1.1 fusion.50
  352.6 1.1 fusion.50
  355.9 1.1 fusion.50
  359.1 1.1 fusion.50
  362.4 1.1 fusion.50
  364.6 1.1 fusion.50
  367.9 1.1 fusion.50
  371.1 1.1 fusion.50
  373.3 1.1 fusion.50
  376.6 1.1 fusion.50
  379.9 1.1 fusion.50
  383.1 1.1 fusion.50
  385.3 1.1 fusion.50
  388.6 1.1 fusion.50
  391.9 1.1 fusion.50
  394.1 1.1 fusion.50
  397.3 1.1 fusion.50
  400.6 1.1 fusion.50
  457.5 40.8 %fusion.3 = (f32[128,4096]{1,0:T(8,128)}, f32[128,4096]{1,0:T(8,128)}, f32[128,4096]{1,0:T(8,128)}, f32[128,4096]{1,0:T(8,128)}) fusion(f32[4,128,4096]{2,1,0:T(8,128)} %copy-done, f32[4,4096]{1,0:T(4,128)S(1)} %copy-done.7, f32[128]{0:T(128)S(1)} %copy-done.16, f32[4,4096]{1,0:T(4,128)S(1)} %get-tuple-element.161, f32[4,4096]{1,0:T(4,128)S(1)} %get-tuple-element.159, ...), kind=kLoop, calls=%fused_computation.7 | loop fusion | flops 31457280 | bytes 25560064 | tf_op jit(solution)/shard_map/reduce_sum | solution.py:74
  498.4 5.5 %fusion.9 = (f32[128]{0:T(128)S(1)}, bf16[128,4096]{1,0:T(8,128)(2,1)S(1)}) fusion(f32[128]{0:T(128)S(1)} %copy-done.19, f32[128,4096]{1,0:T(8,128)} %get-tuple-element.118, f32[128,4096]{1,0:T(8,128)} %get-tuple-element.119, f32[128,4096]{1,0:T(8,128)} %get-tuple-element.117, f32[128,4096]{1,0:T(8,128)} %get-tuple-element.120, ...), kind=kLoop, calls=%fused_computation.20 | loop fusion | flops 12582784 | bytes 25281536 | tf_op jit(solution)/shard_map/reduce_sum | solution.py:100
  503.9 3.2 psum.7
  507.1 1.3 fusion.11
  (169 shorter events, 115.3 us)
Async XLA Ops:
  7.2 19.6 %copy-start.2 = (bf16[128,4096]{1,0:T(8,128)(2,1)S(1)}, bf16[128,4096]{1,0:T(8,128)(2,1)}, u32[]{:S(2)}) copy-start(bf16[128,4096]{1,0:T(8,128)(2,1)} %param.12) | copy-start | bytes 3145732
  7.2 159.6 %all-gather.5.cloned.1.call-start = ((), (), s32[]{:S(2)}) async-start(), calls=%async_computation | async-start | bytes 16908288 | tf_op jit(solution)/shard_map/all_gather | solution.py:15
  9.6 0.6 copy-start.18
  12.6 306.2 %all-gather.7.cloned.1.call-start = ((), (), s32[]{:S(2)}) async-start(), calls=%async_computation.1 | async-start | bytes 16908288 | tf_op jit(solution)/shard_map/all_gather | solution.py:15
  13.5 13.3 %collective-permute-start.1 = (bf16[6,4096]{1,0:T(8,128)(2,1)S(1)}, bf16[6,4096]{1,0:T(8,128)(2,1)S(1)}, u32[]{:S(2)}, u32[]{:S(2)}) collective-permute-start(bf16[6,4096]{1,0:T(8,128)(2,1)S(1)} %slice.235), channel_id=1, source_target_pairs={{0,2},{2,4},{4,6},{6,8},{8,10},{10,12},{12,14},{14,16},{16,18},{18... | collective-permute-start | bytes 147464 | tf_op jit(solution)/shard_map/ppermute | solution.py:10
  18.3 8.8 %collective-permute-start.2 = (bf16[6,4096]{1,0:T(8,128)(2,1)S(1)}, bf16[6,4096]{1,0:T(8,128)(2,1)S(1)}, u32[]{:S(2)}, u32[]{:S(2)}) collective-permute-start(bf16[6,4096]{1,0:T(8,128)(2,1)S(1)} %slice.250), channel_id=1, source_target_pairs={{0,2},{2,4},{4,6},{6,8},{8,10},{10,12},{12,14},{14,16},{16,18},{18... | collective-permute-start | bytes 147464 | tf_op jit(solution)/shard_map/ppermute | solution.py:10
  22.4 4.6 copy-start.3
  26.7 4.2 copy-start.15
  64.9 18.7 %copy-start.4 = (bf16[128,4096]{1,0:T(8,128)(2,1)S(1)}, bf16[128,4096]{1,0:T(8,128)(2,1)}, u32[]{:S(2)}) copy-start(bf16[128,4096]{1,0:T(8,128)(2,1)} %param.11) | copy-start | bytes 3145732
  78.6 3.2 copy-start
  83.6 4.7 collective-permute-start
  89.4 368.0 %copy-start.6 = (f32[4,4096]{1,0:T(4,128)S(1)}, f32[4,4096]{1,0:T(4,128)}, u32[]{:S(2)}) copy-start(f32[4,4096]{1,0:T(4,128)} %get-tuple-element.156) | copy-start | bytes 196612
  89.4 368.0 %copy-start.7 = (f32[4,4096]{1,0:T(4,128)S(1)}, f32[4,4096]{1,0:T(4,128)}, u32[]{:S(2)}) copy-start(f32[4,4096]{1,0:T(4,128)} %get-tuple-element.157) | copy-start | bytes 196612
  89.4 368.0 %copy-start.16 = (f32[128]{0:T(128)S(1)}, f32[128]{0:T(128)}, u32[]{:S(2)}) copy-start(f32[128]{0:T(128)} %copy-done.15) | copy-start | bytes 1540
  89.4 368.0 %copy-start.17 = (f32[128]{0:T(128)S(1)}, f32[128]{0:T(128)}, u32[]{:S(2)}) copy-start(f32[128]{0:T(128)} %add_convert_fusion) | copy-start | bytes 1540
  457.4 40.9 %copy-start.5 = (bf16[128,4096]{1,0:T(8,128)(2,1)S(1)}, bf16[128,4096]{1,0:T(8,128)(2,1)}, u32[]{:S(2)}) copy-start(bf16[128,4096]{1,0:T(8,128)(2,1)} %param.14) | copy-start | bytes 3145732
  457.4 40.9 %copy-start.8 = (f32[1,1,4096]{2,1,0:T(1,128)S(1)}, f32[1,1,4096]{2,1,0:T(1,128)}, u32[]{:S(2)}) copy-start(f32[1,1,4096]{2,1,0:T(1,128)} %get-tuple-element.148) | copy-start | bytes 49156
  457.4 40.9 %copy-start.9 = (f32[1,1,4096]{2,1,0:T(1,128)S(1)}, f32[1,1,4096]{2,1,0:T(1,128)}, u32[]{:S(2)}) copy-start(f32[1,1,4096]{2,1,0:T(1,128)} %get-tuple-element.149) | copy-start | bytes 49156
  457.4 40.9 %copy-start.10 = (f32[1,1,4096]{2,1,0:T(1,128)S(1)}, f32[1,1,4096]{2,1,0:T(1,128)}, u32[]{:S(2)}) copy-start(f32[1,1,4096]{2,1,0:T(1,128)} %get-tuple-element.150) | copy-start | bytes 49156
  457.4 40.9 %copy-start.11 = (f32[1,1,4096]{2,1,0:T(1,128)S(1)}, f32[1,1,4096]{2,1,0:T(1,128)}, u32[]{:S(2)}) copy-start(f32[1,1,4096]{2,1,0:T(1,128)} %get-tuple-element.151) | copy-start | bytes 49156
  457.4 40.9 %copy-start.12 = (f32[1,1,4096]{2,1,0:T(1,128)S(1)}, f32[1,1,4096]{2,1,0:T(1,128)}, u32[]{:S(2)}) copy-start(f32[1,1,4096]{2,1,0:T(1,128)} %get-tuple-element.152) | copy-start | bytes 49156
  457.5 40.9 %copy-start.13 = (f32[1,1,4096]{2,1,0:T(1,128)S(1)}, f32[1,1,4096]{2,1,0:T(1,128)}, u32[]{:S(2)}) copy-start(f32[1,1,4096]{2,1,0:T(1,128)} %get-tuple-element.153) | copy-start | bytes 49156
  457.5 40.9 %copy-start.19 = (f32[128]{0:T(128)S(1)}, f32[128]{0:T(128)}, u32[]{:S(2)}) copy-start(f32[128]{0:T(128)} %copy-done.18) | copy-start | bytes 1540
  498.4 8.7 %copy-start.14 = (f32[4096]{0:T(1024)S(1)}, f32[4096]{0:T(1024)}, u32[]{:S(2)}) copy-start(f32[4096]{0:T(1024)} %param.18) | copy-start | bytes 49156
  503.9 4.5 copy-start.1
Sparse Core Ops, SparseCore 0:
  12.7 153.9 all-gather.4
  171.0 147.7 all-gather.6
where the time goes:
time: 518 us; the launch traced here: 515 us
  waiting for transfers between devices  229 us (44%)
  other arithmetic  207 us (40%)
  matrix products  24.7 us (5%)
  local copies, waits for them, and re-layouts  23.3 us (4%)
  between operations  14.4 us (3%)
  starting transfers between devices  10.6 us (2%)
    all_gather x2, waiting for transfers between devices, carried_in(): pieces = jax.tree.map(lambda part: lax.all_gather(part, axis), value)  229 us
    select_n x127, other arithmetic, turn(): jnp.where(position < mine, new, old)  136 us
    reduce_sum x1, other arithmetic, body(): jnp.sum(coef[lower:lower + group][:, None, :] * fall * summed, axis=0)  40.8 us
    dot_general x2, matrix products, body(): jnp.einsum('ts,gsc->gtc', within, rise * z_prod[None], precision=lax.Prec...  24.7 us
    dot_general x1, local copies, waits for them, and re-layouts, body(): jnp.einsum('ts,gsc->gtc', within, rise * z_prod[None], precision=lax.Prec...  12 us
    exp x1, other arithmetic, body(): fall = jnp.exp(-block_part_rate[:, None, :] * centre[None, :, None])  11 us
    ppermute x3, starting transfers between devices, from_behind(): return lax.ppermute(shard, axis, pairs)  10.5 us
  transfers between devices with their start and end apart: 5, of which 2 were waited for; matrix products, arithmetic and copies ran while one was open for 12% of the time, Pallas kernels for 0%

commit v1 on v0

v1 whole, which is shorter than its diff:
```python
import functools
import jax
import jax.numpy as jnp
from jax import lax
from jax.experimental import pallas as pl
from jax.experimental.pallas import tpu as pltpu
from jax.sharding import PartitionSpec as P

MESH = pl.DeviceIdType.MESH
PLANE = 16
LANES = 128
SUB = 8
F32 = jnp.float32


def kernel(
    dims,
    q_hbm, k_hbm, v_hbm, r_hbm, sf_hbm, residue_hbm, rate_hbm, gain_hbm, seg_ref,
    stream_ref, normed_ref,
    q_in, k_in, v_in, r_in, sf_in, residue_in, rate_in, gain_in,
    rim_q, rim_k, rim_v,
    xq, xk, xv, zs, conv_std, qs_std,
    taps_t, rate_n, coef_n, dec_n, weights, dec8_n,
    keep_m, last_m, carry_m,
    e_loc, e_buf, pre_buf, total_buf, plane_buf, inc_buf, sq_loc, sq_far,
    in_sem, param_sem, rim_send, rim_recv, s1, r1, s2, r2, s3, r3, sq_send, sq_recv,
):
    shards, planes, tok, chans, modes, taps, segs = dims
    blocks = tok // SUB
    tiles = chans // LANES
    groups = tiles // SUB
    wide = SUB * LANES
    part = tiles * modes // PLANE
    me = lax.axis_index("seq")
    core = lax.axis_index("chan")
    zed = me // PLANE
    spot = lax.rem(me, PLANE)
    after = lax.rem(me + 1, shards)
    before = lax.rem(me + shards - 1, shards)

    def at(ref, start, size):
        return ref.at[pl.ds(pl.multiple_of(start, SUB), size)]

    params = [
        pltpu.make_async_copy(rate_hbm, rate_in, param_sem.at[0]),
        pltpu.make_async_copy(sf_hbm, sf_in, param_sem.at[1]),
        pltpu.make_async_copy(residue_hbm, residue_in, param_sem.at[2]),
        pltpu.make_async_copy(gain_hbm, gain_in, param_sem.at[3]),
    ]

    def load(index, src, dst, g):
        cols = pl.ds(g * wide, wide)
        return pltpu.make_async_copy(src.at[:, cols], dst.at[:, cols], in_sem.at[index, g])

    for copy in params[:2]:
        copy.start()
    for g in range(groups):
        load(1, k_hbm, k_in, g).start()
        load(2, v_hbm, v_in, g).start()
    for copy in params[2:]:
        copy.start()
    for g in range(groups):
        load(0, q_hbm, q_in, g).start()
    for g in range(groups):
        load(3, r_hbm, r_in, g).start()

    barrier = pltpu.get_barrier_semaphore()

    @pl.loop(1, PLANE)
    def _(step):
        other = zed * PLANE + lax.rem(spot + step, PLANE)
        pl.semaphore_signal(barrier, inc=1, device_id=(other, core), device_id_type=MESH)

    @pl.loop(1, planes)
    def _(step):
        other = lax.rem(zed + step, planes) * PLANE + spot
        pl.semaphore_signal(barrier, inc=1, device_id=(other, core), device_id_type=MESH)

    pl.semaphore_signal(barrier, inc=1, device_id=(before, core), device_id_type=MESH)
    pl.semaphore_signal(barrier, inc=1, device_id=(me, 1 - core), device_id_type=MESH)

    first = me * tok
    ends = []
    running = seg_ref[0]
    ends.append(running)
    for j in range(1, segs):
        running = running + seg_ref[j]
        ends.append(running)
    big = jnp.int32(1 << 30)
    low = big
    high = jnp.int32(-1)
    for end in ends:
        low = jnp.minimum(low, jnp.where(end >= first, end, big))
        high = jnp.maximum(high, jnp.where(end <= first + tok - 1, end, -1))
    rows = lax.broadcasted_iota(jnp.int32, (tok, LANES), 0) + first
    begins = rows == 0
    for end in ends:
        begins = begins | (rows == end)
    keep_m[...] = jnp.where(begins, 0.0, 1.0)
    last_m[...] = jnp.where(rows >= high, 1.0, 0.0)
    carry_m[...] = jnp.where(rows < low, 1.0, 0.0)

    params[0].wait()
    for t in range(tiles):
        rate = rate_in[:, t * LANES : (t + 1) * LANES]
        rate_n[t * modes : (t + 1) * modes, :] = rate
        dec_n[t * modes : (t + 1) * modes, :] = jnp.exp(-rate)
    params[1].wait()
    for a in range(3):
        for t in range(tiles):
            taps_t[a, t * SUB : t * SUB + taps, :] = sf_in[a, :, t * LANES : (t + 1) * LANES]

    pl.semaphore_wait(barrier, PLANE - 1 + planes - 1 + 2)

    def rim_copy(index, src, dst):
        return pltpu.make_async_remote_copy(
            src_ref=src.at[pl.ds(tok - SUB, SUB)], dst_ref=dst,
            send_sem=rim_send.at[index], recv_sem=rim_recv.at[index],
            device_id=(after, core), device_id_type=MESH,
        )

    rims = [rim_copy(0, k_hbm, rim_k), rim_copy(1, v_hbm, rim_v), rim_copy(2, q_hbm, rim_q)]
    for copy in rims:
        copy.start()

    def row_of(block, tile):
        return (block * tiles + tile) * SUB

    def relayout(src, dst, g):
        @pl.loop(0, blocks // 2)
        def _(pair):
            for j in range(SUB):
                x = src[pl.ds(pl.multiple_of(pair * 2 * SUB, 2 * SUB), 2 * SUB),
                        pl.ds(pl.multiple_of(g * wide + j * LANES, LANES), LANES)].astype(F32)
                lower = pl.multiple_of(row_of(2 * pair + 1, g * SUB + j), SUB)
                dst[pl.ds(lower, SUB), :] = x[:SUB]
                upper = pl.multiple_of(row_of(2 * pair + 2, g * SUB + j), SUB)
                dst[pl.ds(upper, SUB), :] = x[SUB:]

    def relayout_rim(src, dst):
        for t in range(tiles):
            x = src[:, t * LANES : (t + 1) * LANES].astype(F32)
            dst[t * SUB : (t + 1) * SUB, :] = jnp.where(me > 0, x, 0.0)

    def token(ref, block, g, s):
        return ref[pl.ds(row_of(block, g * SUB) + s, SUB, stride=SUB), :]

    def per_mode(ref, g, m):
        return ref[pl.ds(g * SUB * modes + m, SUB, stride=modes), :]

    def taps_of(a, g):
        return [taps_t[a, pl.ds(g * SUB * SUB + j, SUB, stride=SUB), :] for j in range(taps)]

    def fir(window, weight):
        out = weight[0] * window[-1]
        for j in range(1, taps):
            out = out + weight[j] * window[-1 - j]
        return out

    def z_rows(t, g):
        return pl.ds(pl.multiple_of((t * groups + g) * SUB, SUB), SUB)

    def block_of_z(block, g, k_win, v_win, state, k_taps, v_taps, decay):
        k_win, v_win, state = list(k_win), list(v_win), list(state)
        for s in range(SUB):
            k_win.append(token(xk, block, g, s))
            v_win.append(token(xv, block, g, s))
            z = fir(k_win[-taps:], k_taps) * fir(v_win[-taps:], v_taps)
            t = (block - 1) * SUB + s
            zs[z_rows(t, g), :] = z
            z = z * last_m[pl.ds(t, 1), :]
            state = [d * old + z for d, old in zip(decay, state)]
        return k_win[1 - taps :], v_win[1 - taps :], state

    zero = jnp.zeros((SUB, LANES), F32)

    @pl.loop(0, groups)
    def _(g):
        load(1, k_hbm, k_in, g).wait()
        load(2, v_hbm, v_in, g).wait()
        relayout(k_in, xk, g)
        relayout(v_in, xv, g)
        k_taps, v_taps = taps_of(1, g), taps_of(2, g)
        decay = [per_mode(dec_n, g, m) for m in range(modes)]
        behind = range(SUB - taps + 1, SUB)
        start = (
            [token(xk, 1, g, s) for s in behind],
            [token(xv, 1, g, s) for s in behind],
            [zero] * modes,
        )

        def step(block, carried):
            return block_of_z(block, g, *carried, k_taps, v_taps, decay)

        _, _, state = lax.fori_loop(2, blocks + 1, step, start)
        for m in range(modes):
            e_loc[pl.ds(g * SUB * modes + m, SUB, stride=modes), :] = state[m]

    rims[0].wait_recv()
    rims[1].wait_recv()
    relayout_rim(rim_k, xk)
    relayout_rim(rim_v, xv)

    @pl.loop(0, groups)
    def _(g):
        k_taps, v_taps = taps_of(1, g), taps_of(2, g)
        decay = [per_mode(dec_n, g, m) for m in range(modes)]
        behind = range(SUB - taps + 1, SUB)
        _, _, state = block_of_z(
            1, g, [token(xk, 0, g, s) for s in behind], [token(xv, 0, g, s) for s in behind],
            [zero] * modes, k_taps, v_taps, decay,
        )
        for m in range(modes):
            rest = jnp.exp(per_mode(rate_n, g, m) * float(SUB - tok))
            here = pl.ds(g * SUB * modes + m, SUB, stride=modes)
            e_loc[here, :] = e_loc[here, :] + rest * state[m]

    def round_1(other):
        return pltpu.make_async_remote_copy(
            src_ref=at(e_loc, other * part, part), dst_ref=e_buf.at[spot],
            send_sem=s1.at[other], recv_sem=r1.at[spot],
            device_id=(zed * PLANE + other, core), device_id_type=MESH,
        )

    def arrival_1(other):
        return pltpu.make_async_remote_copy(
            src_ref=at(e_loc, other * part, part), dst_ref=e_buf.at[other],
            send_sem=s1.at[other], recv_sem=r1.at[other],
            device_id=(zed * PLANE + other, core), device_id_type=MESH,
        )

    @pl.loop(1, PLANE)
    def _(step):
        round_1(lax.rem(spot + step, PLANE)).start()

    e_buf[spot] = at(e_loc, spot * part, part)[...]

    params[2].wait()
    params[3].wait()
    for t in range(tiles):
        x = -2.0 * rate_n[t * modes : (t + 1) * modes, :]
        series = 1.0 + x * (1.0 / 6.0)
        for n in (5.0, 4.0, 3.0, 2.0):
            series = 1.0 + x * (1.0 / n) * series
        coef_n[t * modes : (t + 1) * modes, :] = residue_in[:, t * LANES : (t + 1) * LANES] * jnp.sqrt(-x * series)

    @pl.loop(0, groups)
    def _(g):
        load(0, q_hbm, q_in, g).wait()
        relayout(q_in, xq, g)

    rims[2].wait_recv()
    relayout_rim(rim_q, xq)

    @pl.loop(1, PLANE)
    def _(step):
        arrival_1(lax.rem(spot + step, PLANE)).wait_recv()

    my_rate = at(rate_n, spot * part, part)[...]
    span = jnp.exp(my_rate * float(-tok))
    spot_rows = lax.broadcasted_iota(jnp.int32, (PLANE, LANES), 0) + zed * PLANE
    plane_rows = lax.broadcasted_iota(jnp.int32, (SUB, LANES), 0)
    open_here = jnp.ones((PLANE, LANES), F32)
    open_plane = jnp.ones((SUB, LANES), F32)
    for end in ends:
        open_here = jnp.where(spot_rows == end // tok, 0.0, open_here)
        open_plane = jnp.where(plane_rows == end // (tok * PLANE), 0.0, open_plane)

    state = jnp.zeros_like(span)
    reach = jnp.ones_like(span)
    reaches = []
    for other in range(PLANE):
        pre_buf[other] = state
        reaches.append(reach)
        factor = span * open_here[other : other + 1]
        state = factor * state + e_buf[other]
        reach = factor * reach
    total_buf[...] = state

    def round_2(there, slot):
        return pltpu.make_async_remote_copy(
            src_ref=total_buf, dst_ref=plane_buf.at[slot],
            send_sem=s2.at[there], recv_sem=r2.at[slot],
            device_id=(there * PLANE + spot, core), device_id_type=MESH,
        )

    @pl.loop(zed + 1, planes)
    def _(there):
        round_2(there, zed).start()

    def inner(g):
        q_taps = taps_of(0, g)
        decay = [per_mode(dec_n, g, m) for m in range(modes)]
        coef = [per_mode(coef_n, g, m) for m in range(modes)]
        behind = range(SUB - taps + 1, SUB)

        def step(block, carried):
            q_win, state = list(carried[0]), list(carried[1])
            for s in range(SUB):
                q_win.append(token(xq, block, g, s))
                qs = fir(q_win[-taps:], q_taps)
                t = (block - 1) * SUB + s
                z = zs[z_rows(t, g), :]
                keep = keep_m[pl.ds(t, 1), :]
                state = [(d * keep) * old + z for d, old in zip(decay, state)]
                out = coef[0] * state[0]
                for m in range(1, modes):
                    out = out + coef[m] * state[m]
                there = pl.ds(row_of(block - 1, g * SUB) + s, SUB, stride=SUB)
                conv_std[there, :] = out
                qs_std[there, :] = qs
            return q_win[1 - taps :], state

        start = ([token(xq, 0, g, s) for s in behind], [zero] * modes)
        lax.fori_loop(1, blocks + 1, step, start)

    @pl.loop(0, groups // 2)
    def _(g):
        inner(g)

    plane_span = jnp.exp(my_rate * float(-tok * PLANE))

    def plane_step(there, state):
        round_2(there, there).wait_recv()
        row = jnp.sum(jnp.where(plane_rows == there, open_plane, 0.0), axis=0, keepdims=True)
        return plane_span * row * state + plane_buf[there]

    state = lax.fori_loop(0, zed, plane_step, jnp.zeros_like(span))
    for other in range(PLANE):
        pre_buf[other] = pre_buf[other] + reaches[other] * state

    def round_3(other, slot):
        return pltpu.make_async_remote_copy(
            src_ref=pre_buf.at[other], dst_ref=inc_buf.at[slot],
            send_sem=s3.at[other], recv_sem=r3.at[slot],
            device_id=(zed * PLANE + other, core), device_id_type=MESH,
        )

    @pl.loop(1, PLANE)
    def _(step):
        round_3(lax.rem(spot + step, PLANE), spot).start()

    inc_buf[spot] = pre_buf[spot]

    @pl.loop(groups // 2, groups)
    def _(g):
        inner(g)

    rising = (lax.broadcasted_iota(jnp.int32, (SUB, LANES), 0) + 1).astype(F32)

    @pl.loop(0, tiles)
    def _(t):
        for m in range(modes):
            rate = rate_n[pl.ds(t * modes + m, 1), :]
            coef = coef_n[pl.ds(t * modes + m, 1), :]
            here = pl.ds(pl.multiple_of((t * modes + m) * SUB, SUB), SUB)
            weights[here, :] = coef * jnp.exp(-rate * rising)
        whole = pl.ds(pl.multiple_of(t * modes, SUB), modes)
        dec8_n[whole, :] = jnp.exp(rate_n[whole, :] * float(-SUB))

    for g in range(groups):
        load(3, r_hbm, r_in, g).wait()

    @pl.loop(1, PLANE)
    def _(step):
        other = lax.rem(spot + step, PLANE)
        round_3(other, other).wait_recv()

    per = tiles // PLANE

    def tile_of(t, squares):
        value, decay = [], []
        for m in range(modes):
            here = pl.ds(pl.multiple_of((t * modes + m) * SUB, SUB), SUB)
            slot = t // per
            row = (t - slot * per) * modes + m
            value.append(weights[here, :] * inc_buf[slot, pl.ds(row, 1), :])
            decay.append(jnp.broadcast_to(dec8_n[pl.ds(t * modes + m, 1), :], (SUB, LANES)))
        cols = pl.ds(pl.multiple_of(t * LANES, LANES), LANES)
        squares = list(squares)
        for pair in range(blocks // 2):
            halves = []
            for block in (2 * pair, 2 * pair + 1):
                carried = value[0]
                for m in range(1, modes):
                    carried = carried + value[m]
                value = [v * d for v, d in zip(value, decay)]
                here = pl.ds(pl.multiple_of(row_of(block, t), SUB), SUB)
                mask = carry_m[block * SUB : (block + 1) * SUB, :]
                halves.append(qs_std[here, :] * (conv_std[here, :] + carried * mask))
            both = pl.ds(pair * 2 * SUB, 2 * SUB)
            stream = (r_in[both, cols].astype(F32) + jnp.concatenate(halves, axis=0)).astype(jnp.bfloat16)
            stream_ref[both, cols] = stream
            back = stream.astype(F32)
            square = back * back
            squares[2 * pair] = squares[2 * pair] + square[:SUB]
            squares[2 * pair + 1] = squares[2 * pair + 1] + square[SUB:]
        return squares

    squares = lax.fori_loop(0, tiles, tile_of, [zero] * blocks)
    for block in range(blocks):
        sq_loc[block * SUB : (block + 1) * SUB, :] = squares[block]

    swap = pltpu.make_async_remote_copy(
        src_ref=sq_loc, dst_ref=sq_far, send_sem=sq_send, recv_sem=sq_recv,
        device_id=(me, 1 - core), device_id_type=MESH,
    )
    swap.start()

    for copy in rims:
        copy.wait_send()

    @pl.loop(1, PLANE)
    def _(step):
        other = lax.rem(spot + step, PLANE)
        round_1(other).wait_send()
        round_3(other, spot).wait_send()

    @pl.loop(zed + 1, planes)
    def _(there):
        round_2(there, zed).wait_send()

    swap.wait()
    total = jnp.sum(sq_loc[...] + sq_far[...], axis=1, keepdims=True)
    scale = lax.rsqrt(total * (1.0 / (2 * chans)) + 1e-6)
    sq_loc[...] = jnp.broadcast_to(scale, (tok, LANES))

    @pl.loop(0, tiles)
    def _(t):
        cols = pl.ds(pl.multiple_of(t * LANES, LANES), LANES)
        gain = gain_in[pl.ds(t, 1), :]
        for pair in range(blocks // 2):
            both = pl.ds(pair * 2 * SUB, 2 * SUB)
            x = stream_ref[both, cols].astype(F32)
            normed_ref[both, cols] = (x * sq_loc[both, :] * gain).astype(jnp.bfloat16)


def body(q_proj, k_proj, v_proj, resid, short_filter, residue, rate, gain, seg_lengths):
    tok, chans = q_proj.shape
    taps = short_filter.shape[1]
    modes = rate.shape[0]
    segs = seg_lengths.shape[0]
    shards = lax.axis_size("seq")
    planes = shards // PLANE
    tiles = chans // LANES
    groups = tiles // SUB
    blocks = tok // SUB
    part = tiles * modes // PLANE
    bf16 = jnp.bfloat16
    dims = (shards, planes, tok, chans, modes, taps, segs)
    vmem = pltpu.VMEM
    sem = pltpu.SemaphoreType.DMA
    any_spec = pl.BlockSpec(memory_space=pl.ANY)
    return pl.pallas_call(
        functools.partial(kernel, dims),
        out_shape=(jax.ShapeDtypeStruct((tok, chans), bf16),) * 2,
        in_specs=[any_spec] * 8 + [pl.BlockSpec(memory_space=pltpu.SMEM)],
        out_specs=(pl.BlockSpec(memory_space=vmem),) * 2,
        scratch_shapes=[
            vmem((tok, chans), bf16), vmem((tok, chans), bf16), vmem((tok, chans), bf16), vmem((tok, chans), bf16),
            vmem((3, taps, chans), F32), vmem((modes, chans), F32), vmem((modes, chans), F32), vmem((tiles, LANES), F32),
            vmem((SUB, chans), bf16), vmem((SUB, chans), bf16), vmem((SUB, chans), bf16),
            vmem(((blocks + 1) * tiles * SUB, LANES), F32),
            vmem(((blocks + 1) * tiles * SUB, LANES), F32),
            vmem(((blocks + 1) * tiles * SUB, LANES), F32),
            vmem((blocks * tiles * SUB, LANES), F32),
            vmem((blocks * tiles * SUB, LANES), F32),
            vmem((blocks * tiles * SUB, LANES), F32),
            vmem((3, tiles * SUB, LANES), F32),
            vmem((tiles * modes, LANES), F32), vmem((tiles * modes, LANES), F32), vmem((tiles * modes, LANES), F32),
            vmem((tiles * modes * SUB, LANES), F32), vmem((tiles * modes, LANES), F32),
            vmem((tok, LANES), F32), vmem((tok, LANES), F32), vmem((tok, LANES), F32),
            vmem((tiles * modes, LANES), F32),
            vmem((PLANE, part, LANES), F32), vmem((PLANE, part, LANES), F32),
            vmem((part, LANES), F32), vmem((planes, part, LANES), F32), vmem((PLANE, part, LANES), F32),
            vmem((tok, LANES), F32), vmem((tok, LANES), F32),
            sem((4, groups)), sem((4,)), sem((3,)), sem((3,)),
            sem((PLANE,)), sem((PLANE,)), sem((planes,)), sem((planes,)), sem((PLANE,)), sem((PLANE,)),
            sem, sem,
        ],
        compiler_params=pltpu.CompilerParams(
            collective_id=0, has_side_effects=True, vmem_limit_bytes=48 * 1024 * 1024
        ),
        name="hyena",
    )(q_proj, k_proj, v_proj, resid, short_filter, residue, rate, gain.reshape(tiles, LANES), seg_lengths)


def solution(mesh):
    placed = (
        P("seq", "chan"),
        P("seq", "chan"),
        P("seq", "chan"),
        P("seq", "chan"),
        P(None, None, "chan"),
        P(None, "chan"),
        P(None, "chan"),
        P("chan"),
        P(),
    )
    return jax.shard_map(
        body,
        mesh=mesh,
        in_specs=placed,
        out_specs=(P("seq", "chan"), P("seq", "chan")),
        check_vma=False,
    )
```

time: 518 us -> 47.5 us (0.09)
  waiting for transfers between devices: 229 us -> 0 us
  other arithmetic: 207 us -> 0 us
  Pallas kernels: 0 us -> 36.7 us
  matrix products: 24.7 us -> 0 us
  between operations: 14.4 us -> 0.66 us
  local copies, waits for them, and re-layouts: 23.3 us -> 9.78 us
  starting transfers between devices: 10.6 us -> 0 us
    all_gather x2 -> x0, waiting for transfers between devices: 229 us -> none  [carried_in(): pieces = jax.tree.map(lambda part: lax.all_gather(part, axis), value)]
    select_n x127 -> x0, other arithmetic: 136 us -> none  [turn(): jnp.where(position < mine, new, old)]
    reduce_sum x4 -> x0, other arithmetic: 47 us -> none  [the longest x1 40.8 us: body(): jnp.sum(coef[lower:lower + group][:, None, :] * fall * summed, axis=0)]
    pallas_call x0 -> x1, Pallas kernels: none -> 36.7 us  [body(): pl.pallas_call(functools.partial(kernel, dims), out_shape=(jax.ShapeDtype...]
    dot_general x2 -> x0, matrix products: 24.7 us -> none  [body(): jnp.einsum('ts,gsc->gtc', within, rise * z_prod[None], precision=lax.Prec...]
    dot_general x1 -> x0, local copies, waits for them, and re-layouts: 12 us -> none  [body(): jnp.einsum('ts,gsc->gtc', within, rise * z_prod[None], precision=lax.Prec...]
    exp x1 -> x0, other arithmetic: 11 us -> none  [body(): fall = jnp.exp(-block_part_rate[:, None, :] * centre[None, :, None])]
    ppermute x3 -> x0, starting transfers between devices: 10.5 us -> none  [from_behind(): return lax.ppermute(shard, axis, pairs)]
  transfers between devices with their start and end apart: 5 -> 0, of which waited for: 2 -> 0; matrix products, arithmetic and copies ran while one was open for 12% -> 0% of each run, Pallas kernels for 0% -> 0%
where the time goes in v1:
time: 47.5 us; the launch traced here: 47.2 us
  Pallas kernels  36.7 us (77%)
  local copies, waits for them, and re-layouts  9.78 us (21%)
  between operations  0.66 us (1%)
    pallas_call x1, Pallas kernels, body(): pl.pallas_call(functools.partial(kernel, dims), out_shape=(jax.ShapeDtype...  36.7 us
    unnamed x18, local copies, waits for them, and re-layouts  9.78 us

profile of v1, /device:TPU:1, one launch (start us, length us, event | category | flops | bytes accessed | tf_op | source)
XLA Modules:
  0.0 47.2 jit_solution(6110187189923803632)
XLA Ops:
  0.6 0.0 copy-start.7
  0.6 0.6 %copy-done.7 = s32[16]{0:T(128)S(1)} copy-done((s32[16]{0:T(128)S(1)}, s32[16]{0:T(128)}, u32[]{:S(2)}) %copy-start.7) | copy-done | bytes 88
  1.3 0.0 copy-start
  1.3 1.2 %copy-done = bf16[128,4096]{1,0:T(8,128)(2,1)S(1)} copy-done((bf16[128,4096]{1,0:T(8,128)(2,1)S(1)}, bf16[128,4096]{1,0:T(8,128)(2,1)}, u32[]{:S(2)}) %copy-start) | copy-done | bytes 1048600
  2.5 0.0 copy-start.1
  2.5 1.2 %copy-done.1 = bf16[128,4096]{1,0:T(8,128)(2,1)S(1)} copy-done((bf16[128,4096]{1,0:T(8,128)(2,1)S(1)}, bf16[128,4096]{1,0:T(8,128)(2,1)}, u32[]{:S(2)}) %copy-start.1) | copy-done | bytes 1048600
  3.7 0.0 copy-start.2
  3.7 1.2 %copy-done.2 = bf16[128,4096]{1,0:T(8,128)(2,1)S(1)} copy-done((bf16[128,4096]{1,0:T(8,128)(2,1)S(1)}, bf16[128,4096]{1,0:T(8,128)(2,1)}, u32[]{:S(2)}) %copy-start.2) | copy-done | bytes 1048600
  5.0 0.0 copy-start.3
  5.0 1.0 %copy-done.3 = f32[3,7,4096]{2,1,0:T(8,128)S(1)} copy-done((f32[3,7,4096]{2,1,0:T(8,128)S(1)}, f32[3,7,4096]{2,1,0:T(8,128)}, u32[]{:S(2)}) %copy-start.3) | copy-done | bytes 344088
  6.0 0.0 copy-start.4
  6.0 0.9 %copy-done.4 = f32[8,4096]{1,0:T(8,128)S(1)} copy-done((f32[8,4096]{1,0:T(8,128)S(1)}, f32[8,4096]{1,0:T(8,128)}, u32[]{:S(2)}) %copy-start.4) | copy-done | bytes 131096
  6.9 0.0 copy-start.5
  6.9 0.9 %copy-done.5 = f32[8,4096]{1,0:T(8,128)S(1)} copy-done((f32[8,4096]{1,0:T(8,128)S(1)}, f32[8,4096]{1,0:T(8,128)}, u32[]{:S(2)}) %copy-start.5) | copy-done | bytes 131096
  7.8 0.0 copy-start.6
  7.8 0.7 %copy-done.6 = f32[4096]{0:T(1024)S(1)} copy-done((f32[4096]{0:T(1024)S(1)}, f32[4096]{0:T(1024)}, u32[]{:S(2)}) %copy-start.6) | copy-done | bytes 16408
  8.5 36.7 %hyena.1 = (bf16[128,4096]{1,0:T(8,128)(2,1)S(1)}, bf16[128,4096]{1,0:T(8,128)(2,1)S(1)}) custom-call(bf16[128,4096]{1,0:T(8,128)(2,1)S(1)} %copy-done, bf16[128,4096]{1,0:T(8,128)(2,1)S(1)} %copy-done.1, bf16[128,4096]{1,0:T(8,128)(2,1)S(1)} %copy-done.2, bf16[128,4096]{1,0:T(8,128)(2,1)} %r_hbm.1, f32[3,7,4096]{2,1,0:T(8,128)S(1)} %copy-done.3, ...), custom_call_target="tpu_custom_call" | custom-call | tf_op jit(solution)/shard_map/hyena/pallas_call | solution.py:454
  45.2 1.0 %copy.13 = bf16[128,4096]{1,0:T(8,128)(2,1)} copy(bf16[128,4096]{1,0:T(8,128)(2,1)S(1)} %get-tuple-element.4) | data formatting | bytes 2097152
  46.2 1.0 %copy.14 = bf16[128,4096]{1,0:T(8,128)(2,1)} copy(bf16[128,4096]{1,0:T(8,128)(2,1)S(1)} %get-tuple-element.5) | data formatting | bytes 2097152
Async XLA Ops:
  0.6 0.7 %copy-start.7 = (s32[16]{0:T(128)S(1)}, s32[16]{0:T(128)}, u32[]{:S(2)}) copy-start(s32[16]{0:T(128)} %seg_ref.1) | copy-start | bytes 196
  1.3 1.2 %copy-start = (bf16[128,4096]{1,0:T(8,128)(2,1)S(1)}, bf16[128,4096]{1,0:T(8,128)(2,1)}, u32[]{:S(2)}) copy-start(bf16[128,4096]{1,0:T(8,128)(2,1)} %q_hbm.1) | copy-start | bytes 3145732
  2.5 1.2 %copy-start.1 = (bf16[128,4096]{1,0:T(8,128)(2,1)S(1)}, bf16[128,4096]{1,0:T(8,128)(2,1)}, u32[]{:S(2)}) copy-start(bf16[128,4096]{1,0:T(8,128)(2,1)} %k_hbm.1) | copy-start | bytes 3145732
  3.7 1.2 %copy-start.2 = (bf16[128,4096]{1,0:T(8,128)(2,1)S(1)}, bf16[128,4096]{1,0:T(8,128)(2,1)}, u32[]{:S(2)}) copy-start(bf16[128,4096]{1,0:T(8,128)(2,1)} %v_hbm.1) | copy-start | bytes 3145732
  5.0 1.0 %copy-start.3 = (f32[3,7,4096]{2,1,0:T(8,128)S(1)}, f32[3,7,4096]{2,1,0:T(8,128)}, u32[]{:S(2)}) copy-start(f32[3,7,4096]{2,1,0:T(8,128)} %sf_hbm.1) | copy-start | bytes 1032196
  6.0 0.9 %copy-start.4 = (f32[8,4096]{1,0:T(8,128)S(1)}, f32[8,4096]{1,0:T(8,128)}, u32[]{:S(2)}) copy-start(f32[8,4096]{1,0:T(8,128)} %residue_hbm.1) | copy-start | bytes 393220
  6.9 0.9 %copy-start.5 = (f32[8,4096]{1,0:T(8,128)S(1)}, f32[8,4096]{1,0:T(8,128)}, u32[]{:S(2)}) copy-start(f32[8,4096]{1,0:T(8,128)} %rate_hbm.1) | copy-start | bytes 393220
  7.8 0.7 %copy-start.6 = (f32[4096]{0:T(1024)S(1)}, f32[4096]{0:T(1024)}, u32[]{:S(2)}) copy-start(f32[4096]{0:T(1024)} %param.16) | copy-start | bytes 49156

commit v2 on v1

--- a/solution.py
+++ b/solution.py
@@ -15,18 +15,19 @@
 
 def kernel(
     dims,
-    q_hbm, k_hbm, v_hbm, r_hbm, sf_hbm, residue_hbm, rate_hbm, gain_hbm, seg_ref,
-    stream_ref, normed_ref,
-    q_in, k_in, v_in, r_in, sf_in, residue_in, rate_in, gain_in,
+    q_hbm, k_hbm, v_hbm, r_hbm, sf_hbm, residue_hbm, rate_hbm, gain_hbm, seg_hbm,
+    stream_ref, scale_ref, gain_in,
+    q_in, k_in, v_in, r_in, sf_in, residue_in, rate_in, seg_ref,
     rim_q, rim_k, rim_v,
     xq, xk, xv, zs, conv_std, qs_std,
     taps_t, rate_n, coef_n, dec_n, weights, dec8_n,
     keep_m, last_m, carry_m,
-    e_loc, e_buf, pre_buf, total_buf, plane_buf, inc_buf, sq_loc, sq_far,
+    e_loc, e_buf, pre_buf, reach_buf, total_buf, plane_buf, inc_buf, sq_loc, sq_far,
     in_sem, param_sem, rim_send, rim_recv, s1, r1, s2, r2, s3, r3, sq_send, sq_recv,
 ):
     shards, planes, tok, chans, modes, taps, segs = dims
     blocks = tok // SUB
+    pairs = blocks // 2
     tiles = chans // LANES
     groups = tiles // SUB
     wide = SUB * LANES
@@ -46,19 +47,20 @@
         pltpu.make_async_copy(sf_hbm, sf_in, param_sem.at[1]),
         pltpu.make_async_copy(residue_hbm, residue_in, param_sem.at[2]),
         pltpu.make_async_copy(gain_hbm, gain_in, param_sem.at[3]),
+        pltpu.make_async_copy(seg_hbm, seg_ref, param_sem.at[4]),
     ]
 
     def load(index, src, dst, g):
         cols = pl.ds(g * wide, wide)
         return pltpu.make_async_copy(src.at[:, cols], dst.at[:, cols], in_sem.at[index, g])
 
-    for copy in params[:2]:
-        copy.start()
+    for index in (4, 0, 1):
+        params[index].start()
     for g in range(groups):
         load(1, k_hbm, k_in, g).start()
         load(2, v_hbm, v_in, g).start()
-    for copy in params[2:]:
-        copy.start()
+    for index in (2, 3):
+        params[index].start()
     for g in range(groups):
         load(0, q_hbm, q_in, g).start()
     for g in range(groups):
@@ -79,6 +81,7 @@
     pl.semaphore_signal(barrier, inc=1, device_id=(before, core), device_id_type=MESH)
     pl.semaphore_signal(barrier, inc=1, device_id=(me, 1 - core), device_id_type=MESH)
 
+    params[4].wait()
     first = me * tok
     ends = []
     running = seg_ref[0]
@@ -93,10 +96,6 @@
         low = jnp.minimum(low, jnp.where(end >= first, end, big))
         high = jnp.maximum(high, jnp.where(end <= first + tok - 1, end, -1))
     rows = lax.broadcasted_iota(jnp.int32, (tok, LANES), 0) + first
-    begins = rows == 0
-    for end in ends:
-        begins = begins | (rows == end)
-    keep_m[...] = jnp.where(begins, 0.0, 1.0)
     last_m[...] = jnp.where(rows >= high, 1.0, 0.0)
     carry_m[...] = jnp.where(rows < low, 1.0, 0.0)
 
@@ -106,7 +105,7 @@
         rate_n[t * modes : (t + 1) * modes, :] = rate
         dec_n[t * modes : (t + 1) * modes, :] = jnp.exp(-rate)
     params[1].wait()
-    for a in range(3):
+    for a in (1, 2):
         for t in range(tiles):
             taps_t[a, t * SUB : t * SUB + taps, :] = sf_in[a, :, t * LANES : (t + 1) * LANES]
 
@@ -126,16 +125,19 @@
     def row_of(block, tile):
         return (block * tiles + tile) * SUB
 
+    def relayout_tile(src, dst, g, pair, j):
+        x = src[pl.ds(pl.multiple_of(pair * 2 * SUB, 2 * SUB), 2 * SUB),
+                pl.ds(pl.multiple_of(g * wide + j * LANES, LANES), LANES)].astype(F32)
+        lower = pl.multiple_of(row_of(2 * pair + 1, g * SUB + j), SUB)
+        dst[pl.ds(lower, SUB), :] = x[:SUB]
+        upper = pl.multiple_of(row_of(2 * pair + 2, g * SUB + j), SUB)
+        dst[pl.ds(upper, SUB), :] = x[SUB:]
+
     def relayout(src, dst, g):
-        @pl.loop(0, blocks // 2)
+        @pl.loop(0, pairs)
         def _(pair):
             for j in range(SUB):
-                x = src[pl.ds(pl.multiple_of(pair * 2 * SUB, 2 * SUB), 2 * SUB),
-                        pl.ds(pl.multiple_of(g * wide + j * LANES, LANES), LANES)].astype(F32)
-                lower = pl.multiple_of(row_of(2 * pair + 1, g * SUB + j), SUB)
-                dst[pl.ds(lower, SUB), :] = x[:SUB]
-                upper = pl.multiple_of(row_of(2 * pair + 2, g * SUB + j), SUB)
-                dst[pl.ds(upper, SUB), :] = x[SUB:]
+                relayout_tile(src, dst, g, pair, j)
 
     def relayout_rim(src, dst):
         for t in range(tiles):
@@ -160,9 +162,11 @@
     def z_rows(t, g):
         return pl.ds(pl.multiple_of((t * groups + g) * SUB, SUB), SUB)
 
-    def block_of_z(block, g, k_win, v_win, state, k_taps, v_taps, decay):
+    def block_of_z(block, g, k_win, v_win, state, k_taps, v_taps, decay, beside=None):
         k_win, v_win, state = list(k_win), list(v_win), list(state)
         for s in range(SUB):
+            if beside is not None:
+                beside(s)
             k_win.append(token(xk, block, g, s))
             v_win.append(token(xv, block, g, s))
             z = fir(k_win[-taps:], k_taps) * fir(v_win[-taps:], v_taps)
@@ -174,25 +178,49 @@
 
     zero = jnp.zeros((SUB, LANES), F32)
 
+    load(1, k_hbm, k_in, 0).wait()
+    load(2, v_hbm, v_in, 0).wait()
+    for j in range(SUB):
+        relayout_tile(k_in, xk, 0, 0, j)
+        relayout_tile(v_in, xv, 0, 0, j)
+
+    for g in range(groups - 1):
+        load(1, k_hbm, k_in, g + 1).wait()
+        load(2, v_hbm, v_in, g + 1).wait()
+
     @pl.loop(0, groups)
     def _(g):
-        load(1, k_hbm, k_in, g).wait()
-        load(2, v_hbm, v_in, g).wait()
-        relayout(k_in, xk, g)
-        relayout(v_in, xv, g)
         k_taps, v_taps = taps_of(1, g), taps_of(2, g)
         decay = [per_mode(dec_n, g, m) for m in range(modes)]
         behind = range(SUB - taps + 1, SUB)
-        start = (
-            [token(xk, 1, g, s) for s in behind],
-            [token(xv, 1, g, s) for s in behind],
-            [zero] * modes,
-        )
-
-        def step(block, carried):
-            return block_of_z(block, g, *carried, k_taps, v_taps, decay)
-
-        _, _, state = lax.fori_loop(2, blocks + 1, step, start)
+
+        def ahead(pair, half):
+            after_it = jnp.minimum(g * pairs + pair + 1, groups * pairs - 1)
+            g_next, pair_next = after_it // pairs, lax.rem(after_it, pairs)
+
+            def one(s):
+                src, dst = ((k_in, xk), (v_in, xv))[s % 2]
+                if half is None:
+                    relayout_tile(k_in, xk, g_next, pair_next, s)
+                    relayout_tile(v_in, xv, g_next, pair_next, s)
+                else:
+                    relayout_tile(src, dst, g_next, pair_next, half * SUB // 2 + s // 2)
+
+            return one
+
+        start = block_of_z(
+            2, g, [token(xk, 1, g, s) for s in behind], [token(xv, 1, g, s) for s in behind],
+            [zero] * modes, k_taps, v_taps, decay, ahead(0, None),
+        )
+
+        def step(pair, carried):
+            for half in range(2):
+                carried = block_of_z(
+                    2 * pair + 1 + half, g, *carried, k_taps, v_taps, decay, ahead(pair, half)
+                )
+            return carried
+
+        _, _, state = lax.fori_loop(1, pairs, step, start)
         for m in range(modes):
             e_loc[pl.ds(g * SUB * modes + m, SUB, stride=modes), :] = state[m]
 
@@ -229,12 +257,29 @@
             device_id=(zed * PLANE + other, core), device_id_type=MESH,
         )
 
+    side = 4
+
+    def nth(i, j):
+        near = lambda n: (n * (n + 1) // 2) % side
+        y = lax.rem(spot // side + near(i), side)
+        x = lax.rem(spot + near(j), side)
+        return y * side + x
+
+    def nth_of(n):
+        return nth(n // side, lax.rem(n, side))
+
     @pl.loop(1, PLANE)
     def _(step):
-        round_1(lax.rem(spot + step, PLANE)).start()
+        round_1(nth_of(PLANE - step)).start()
 
     e_buf[spot] = at(e_loc, spot * part, part)[...]
 
+    begins = rows == 0
+    for end in ends:
+        begins = begins | (rows == end)
+    keep_m[...] = jnp.where(begins, 0.0, 1.0)
+    for t in range(tiles):
+        taps_t[0, t * SUB : t * SUB + taps, :] = sf_in[0, :, t * LANES : (t + 1) * LANES]
     params[2].wait()
     params[3].wait()
     for t in range(tiles):
@@ -268,10 +313,9 @@
 
     state = jnp.zeros_like(span)
     reach = jnp.ones_like(span)
-    reaches = []
     for other in range(PLANE):
         pre_buf[other] = state
-        reaches.append(reach)
+        reach_buf[other] = reach
         factor = span * open_here[other : other + 1]
         state = factor * state + e_buf[other]
         reach = factor * reach
@@ -307,8 +351,8 @@
                 for m in range(1, modes):
                     out = out + coef[m] * state[m]
                 there = pl.ds(row_of(block - 1, g * SUB) + s, SUB, stride=SUB)
-                conv_std[there, :] = out
-                qs_std[there, :] = qs
+                conv_std[there, :] = out * qs
+                qs_std[there, :] = qs * carry_m[pl.ds(t, 1), :]
             return q_win[1 - taps :], state
 
         start = ([token(xq, 0, g, s) for s in behind], [zero] * modes)
@@ -326,9 +370,6 @@
         return plane_span * row * state + plane_buf[there]
 
     state = lax.fori_loop(0, zed, plane_step, jnp.zeros_like(span))
-    for other in range(PLANE):
-        pre_buf[other] = pre_buf[other] + reaches[other] * state
-
     def round_3(other, slot):
         return pltpu.make_async_remote_copy(
             src_ref=pre_buf.at[other], dst_ref=inc_buf.at[slot],
@@ -338,9 +379,11 @@
 
     @pl.loop(1, PLANE)
     def _(step):
-        round_3(lax.rem(spot + step, PLANE), spot).start()
-
-    inc_buf[spot] = pre_buf[spot]
+        other = nth_of(PLANE - step)
+        pre_buf[other] = pre_buf[other] + reach_buf[other] * state
+        round_3(other, spot).start()
+
+    inc_buf[spot] = pre_buf[spot] + reach_buf[spot] * state
 
     @pl.loop(groups // 2, groups)
     def _(g):
@@ -361,45 +404,56 @@
     for g in range(groups):
         load(3, r_hbm, r_in, g).wait()
 
-    @pl.loop(1, PLANE)
-    def _(step):
-        other = lax.rem(spot + step, PLANE)
-        round_3(other, other).wait_recv()
+    @pl.loop(0, tiles)
+    def _(t):
+        cols = pl.ds(pl.multiple_of(t * LANES, LANES), LANES)
+        for pair in range(pairs):
+            x = r_in[pair * 2 * SUB : (pair + 1) * 2 * SUB, cols].astype(F32)
+            for half in range(2):
+                here = pl.ds(pl.multiple_of(row_of(2 * pair + half, t), SUB), SUB)
+                conv_std[here, :] = conv_std[here, :] + x[half * SUB : (half + 1) * SUB]
+
+    sq_loc[...] = jnp.zeros_like(sq_loc)
 
     per = tiles // PLANE
 
-    def tile_of(t, squares):
+    def tree(terms):
+        while len(terms) > 1:
+            terms = [a + b for a, b in zip(terms[::2], terms[1::2])]
+        return terms[0]
+
+    def tile_of(slot, local):
+        t = slot * per + local
         value, decay = [], []
         for m in range(modes):
             here = pl.ds(pl.multiple_of((t * modes + m) * SUB, SUB), SUB)
-            slot = t // per
-            row = (t - slot * per) * modes + m
-            value.append(weights[here, :] * inc_buf[slot, pl.ds(row, 1), :])
+            value.append(weights[here, :] * inc_buf[slot, pl.ds(local * modes + m, 1), :])
             decay.append(jnp.broadcast_to(dec8_n[pl.ds(t * modes + m, 1), :], (SUB, LANES)))
         cols = pl.ds(pl.multiple_of(t * LANES, LANES), LANES)
-        squares = list(squares)
-        for pair in range(blocks // 2):
+        for pair in range(pairs):
             halves = []
             for block in (2 * pair, 2 * pair + 1):
-                carried = value[0]
-                for m in range(1, modes):
-                    carried = carried + value[m]
-                value = [v * d for v, d in zip(value, decay)]
+                carried = tree(value)
+                if block < blocks - 1:
+                    value = [v * d for v, d in zip(value, decay)]
                 here = pl.ds(pl.multiple_of(row_of(block, t), SUB), SUB)
-                mask = carry_m[block * SUB : (block + 1) * SUB, :]
-                halves.append(qs_std[here, :] * (conv_std[here, :] + carried * mask))
+                halves.append(conv_std[here, :] + qs_std[here, :] * carried)
             both = pl.ds(pair * 2 * SUB, 2 * SUB)
-            stream = (r_in[both, cols].astype(F32) + jnp.concatenate(halves, axis=0)).astype(jnp.bfloat16)
+            stream = jnp.concatenate(halves, axis=0).astype(jnp.bfloat16)
             stream_ref[both, cols] = stream
             back = stream.astype(F32)
-            square = back * back
-            squares[2 * pair] = squares[2 * pair] + square[:SUB]
-            squares[2 * pair + 1] = squares[2 * pair + 1] + square[SUB:]
-        return squares
-
-    squares = lax.fori_loop(0, tiles, tile_of, [zero] * blocks)
-    for block in range(blocks):
-        sq_loc[block * SUB : (block + 1) * SUB, :] = squares[block]
+            sq_loc[both, :] = sq_loc[both, :] + back * back
+
+    @pl.loop(0, PLANE)
+    def _(n):
+        slot = nth_of(n)
+
+        @pl.when(n > 0)
+        def _():
+            round_3(slot, slot).wait_recv()
+
+        for local in range(per):
+            tile_of(slot, local)
 
     swap = pltpu.make_async_remote_copy(
         src_ref=sq_loc, dst_ref=sq_far, send_sem=sq_send, recv_sem=sq_recv,
@@ -423,16 +477,31 @@
     swap.wait()
     total = jnp.sum(sq_loc[...] + sq_far[...], axis=1, keepdims=True)
     scale = lax.rsqrt(total * (1.0 / (2 * chans)) + 1e-6)
-    sq_loc[...] = jnp.broadcast_to(scale, (tok, LANES))
-
-    @pl.loop(0, tiles)
-    def _(t):
-        cols = pl.ds(pl.multiple_of(t * LANES, LANES), LANES)
-        gain = gain_in[pl.ds(t, 1), :]
-        for pair in range(blocks // 2):
-            both = pl.ds(pair * 2 * SUB, 2 * SUB)
-            x = stream_ref[both, cols].astype(F32)
-            normed_ref[both, cols] = (x * sq_loc[both, :] * gain).astype(jnp.bfloat16)
+    scale_ref[...] = jnp.broadcast_to(scale, (tok, LANES))
+
+
+def finish(tok, chans, stream_ref, scale_ref, gain_ref, stream_hbm, normed_hbm, normed, sem):
+    wide = SUB * LANES
+    groups = chans // wide
+    copies = [pltpu.make_async_copy(stream_ref, stream_hbm, sem.at[groups])]
+    copies[0].start()
+    for g in range(groups):
+        for t in range(g * SUB, (g + 1) * SUB):
+            cols = slice(t * LANES, (t + 1) * LANES)
+            gain = gain_ref[t : t + 1, :]
+
+            @pl.loop(0, tok // (2 * SUB))
+            def _(pair):
+                both = pl.ds(pl.multiple_of(pair * 2 * SUB, 2 * SUB), 2 * SUB)
+                x = stream_ref[both, cols].astype(F32)
+                normed[both, cols] = (x * scale_ref[both, :] * gain).astype(jnp.bfloat16)
+
+        part = slice(g * wide, (g + 1) * wide)
+        copy = pltpu.make_async_copy(normed.at[:, part], normed_hbm.at[:, part], sem.at[g])
+        copy.start()
+        copies.append(copy)
+    for copy in copies:
+        copy.wait()
 
 
 def body(q_proj, k_proj, v_proj, resid, short_filter, residue, rate, gain, seg_lengths):
@@ -450,15 +519,20 @@
     dims = (shards, planes, tok, chans, modes, taps, segs)
     vmem = pltpu.VMEM
     sem = pltpu.SemaphoreType.DMA
-    any_spec = pl.BlockSpec(memory_space=pl.ANY)
-    return pl.pallas_call(
+    hbm_spec = pl.BlockSpec(memory_space=pltpu.HBM)
+    stream, scale, gain = pl.pallas_call(
         functools.partial(kernel, dims),
-        out_shape=(jax.ShapeDtypeStruct((tok, chans), bf16),) * 2,
-        in_specs=[any_spec] * 8 + [pl.BlockSpec(memory_space=pltpu.SMEM)],
-        out_specs=(pl.BlockSpec(memory_space=vmem),) * 2,
+        out_shape=(
+            jax.ShapeDtypeStruct((tok, chans), bf16),
+            jax.ShapeDtypeStruct((tok, LANES), F32),
+            jax.ShapeDtypeStruct((tiles, LANES), F32),
+        ),
+        in_specs=[hbm_spec] * 9,
+        out_specs=(pl.BlockSpec(memory_space=vmem),) * 3,
         scratch_shapes=[
             vmem((tok, chans), bf16), vmem((tok, chans), bf16), vmem((tok, chans), bf16), vmem((tok, chans), bf16),
-            vmem((3, taps, chans), F32), vmem((modes, chans), F32), vmem((modes, chans), F32), vmem((tiles, LANES), F32),
+            vmem((3, taps, chans), F32), vmem((modes, chans), F32), vmem((modes, chans), F32),
+            pltpu.SMEM((segs,), jnp.int32),
             vmem((SUB, chans), bf16), vmem((SUB, chans), bf16), vmem((SUB, chans), bf16),
             vmem(((blocks + 1) * tiles * SUB, LANES), F32),
             vmem(((blocks + 1) * tiles * SUB, LANES), F32),
@@ -471,18 +545,29 @@
             vmem((tiles * modes * SUB, LANES), F32), vmem((tiles * modes, LANES), F32),
             vmem((tok, LANES), F32), vmem((tok, LANES), F32), vmem((tok, LANES), F32),
             vmem((tiles * modes, LANES), F32),
-            vmem((PLANE, part, LANES), F32), vmem((PLANE, part, LANES), F32),
+            vmem((PLANE, part, LANES), F32), vmem((PLANE, part, LANES), F32), vmem((PLANE, part, LANES), F32),
             vmem((part, LANES), F32), vmem((planes, part, LANES), F32), vmem((PLANE, part, LANES), F32),
             vmem((tok, LANES), F32), vmem((tok, LANES), F32),
-            sem((4, groups)), sem((4,)), sem((3,)), sem((3,)),
+            sem((4, groups)), sem((5,)), sem((3,)), sem((3,)),
             sem((PLANE,)), sem((PLANE,)), sem((planes,)), sem((planes,)), sem((PLANE,)), sem((PLANE,)),
             sem, sem,
         ],
         compiler_params=pltpu.CompilerParams(
-            collective_id=0, has_side_effects=True, vmem_limit_bytes=48 * 1024 * 1024
+            collective_id=0, has_side_effects=True, vmem_limit_bytes=40 * 1024 * 1024
         ),
         name="hyena",
-    )(q_proj, k_proj, v_proj, resid, short_filter, residue, rate, gain.reshape(tiles, LANES), seg_lengths)
+    )(*(pltpu.with_memory_space_constraint(x, pltpu.HBM) for x in (
+        q_proj, k_proj, v_proj, resid, short_filter, residue, rate, gain.reshape(tiles, LANES), seg_lengths
+    )))
+    return pl.pallas_call(
+        functools.partial(finish, tok, chans),
+        out_shape=(jax.ShapeDtypeStruct((tok, chans), bf16),) * 2,
+        in_specs=[pl.BlockSpec(memory_space=vmem)] * 3,
+        out_specs=(hbm_spec,) * 2,
+        scratch_shapes=[vmem((tok, chans), bf16), sem((chans // (SUB * LANES) + 1,))],
+        compiler_params=pltpu.CompilerParams(vmem_limit_bytes=16 * 1024 * 1024),
+        name="finish",
+    )(stream, scale, gain)
 
 
 def solution(mesh):

time: 47.5 us -> 37.1 us (0.78)
  local copies, waits for them, and re-layouts: 9.78 us -> 0 us
    unnamed x18 -> x0, local copies, waits for them, and re-layouts: 9.78 us -> none
    pallas_call x1, Pallas kernels: 36.7 us -> 33.5 us  [body(): pl.pallas_call(functools.partial(kernel, dims), out_shape=(jax.ShapeDtype...]
    pallas_call x0 -> x1, Pallas kernels: none -> 2.77 us  [body(): pl.pallas_call(functools.partial(finish, tok, chans), out_shape=(jax.Shap...]
where the time goes in v2:
time: 37.1 us; the launch traced here: 37 us
  Pallas kernels  36.3 us (98%)
  between operations  0.64 us (2%)
    pallas_call x1, Pallas kernels, body(): pl.pallas_call(functools.partial(kernel, dims), out_shape=(jax.ShapeDtype...  33.5 us
    pallas_call x1, Pallas kernels, body(): pl.pallas_call(functools.partial(finish, tok, chans), out_shape=(jax.Shap...  2.77 us

profile of v2, /device:TPU:1, one launch (start us, length us, event | category | flops | bytes accessed | tf_op | source)
XLA Modules:
  0.0 37.0 jit_solution(5157789090382284899)
XLA Ops:
  0.6 33.5 %hyena.1 = (bf16[128,4096]{1,0:T(8,128)(2,1)S(1)}, f32[128,128]{1,0:T(8,128)S(1)}, f32[32,128]{1,0:T(8,128)S(1)}) custom-call(bf16[128,4096]{1,0:T(8,128)(2,1)} %q_hbm.1, bf16[128,4096]{1,0:T(8,128)(2,1)} %k_hbm.1, bf16[128,4096]{1,0:T(8,128)(2,1)} %v_hbm.1, bf16[128,4096]{1,0:T(8,128)(2,1)} %r_hbm.1, f32[3,7,4096]{2,1,0:T(8,128)} %sf_hbm.1, ...), custom_call_target="tpu_custom_call" | custom-call | tf_op jit(solution)/shard_map/hyena/pallas_call | solution.py:523
  34.2 2.8 %finish.1 = (bf16[128,4096]{1,0:T(8,128)(2,1)}, bf16[128,4096]{1,0:T(8,128)(2,1)}) custom-call(bf16[128,4096]{1,0:T(8,128)(2,1)S(1)} %get-tuple-element.5.stream_ref, f32[128,128]{1,0:T(8,128)S(1)} %get-tuple-element.6.scale_ref, f32[32,128]{1,0:T(8,128)S(1)} %get-tuple-element.7.gain_ref), custom_call_target="tpu_custom_call" | custom-call | tf_op jit(solution)/shard_map/finish/pallas_call | solution.py:562

commit v3 on v2

--- a/solution.py
+++ b/solution.py
@@ -18,12 +18,12 @@
     q_hbm, k_hbm, v_hbm, r_hbm, sf_hbm, residue_hbm, rate_hbm, gain_hbm, seg_hbm,
     stream_ref, scale_ref, gain_in,
     q_in, k_in, v_in, r_in, sf_in, residue_in, rate_in, seg_ref,
-    rim_q, rim_k, rim_v,
+    rim_q, rim_k, rim_v, edge, edges, ek, ev, e_first, dec_own, taps_own,
     xq, xk, xv, zs, conv_std, qs_std,
     taps_t, rate_n, coef_n, dec_n, weights, dec8_n,
     keep_m, last_m, carry_m,
     e_loc, e_buf, pre_buf, reach_buf, total_buf, plane_buf, inc_buf, sq_loc, sq_far,
-    in_sem, param_sem, rim_send, rim_recv, s1, r1, s2, r2, s3, r3, sq_send, sq_recv,
+    in_sem, param_sem, rim_send, rim_recv, edge_send, edge_recv, s1, r1, s2, r2, s3, r3, sq_send, sq_recv,
 ):
     shards, planes, tok, chans, modes, taps, segs = dims
     blocks = tok // SUB
@@ -77,6 +77,11 @@
     def _(step):
         other = lax.rem(zed + step, planes) * PLANE + spot
         pl.semaphore_signal(barrier, inc=1, device_id=(other, core), device_id_type=MESH)
+
+    @pl.when(zed > 0)
+    def _():
+        last = (zed - 1) * PLANE + PLANE - 1
+        pl.semaphore_signal(barrier, inc=1, device_id=(last, core), device_id_type=MESH)
 
     pl.semaphore_signal(barrier, inc=1, device_id=(before, core), device_id_type=MESH)
     pl.semaphore_signal(barrier, inc=1, device_id=(me, 1 - core), device_id_type=MESH)
@@ -109,19 +114,6 @@
         for t in range(tiles):
             taps_t[a, t * SUB : t * SUB + taps, :] = sf_in[a, :, t * LANES : (t + 1) * LANES]
 
-    pl.semaphore_wait(barrier, PLANE - 1 + planes - 1 + 2)
-
-    def rim_copy(index, src, dst):
-        return pltpu.make_async_remote_copy(
-            src_ref=src.at[pl.ds(tok - SUB, SUB)], dst_ref=dst,
-            send_sem=rim_send.at[index], recv_sem=rim_recv.at[index],
-            device_id=(after, core), device_id_type=MESH,
-        )
-
-    rims = [rim_copy(0, k_hbm, rim_k), rim_copy(1, v_hbm, rim_v), rim_copy(2, q_hbm, rim_q)]
-    for copy in rims:
-        copy.start()
-
     def row_of(block, tile):
         return (block * tiles + tile) * SUB
 
@@ -188,8 +180,7 @@
         load(1, k_hbm, k_in, g + 1).wait()
         load(2, v_hbm, v_in, g + 1).wait()
 
-    @pl.loop(0, groups)
-    def _(g):
+    def end_states(g):
         k_taps, v_taps = taps_of(1, g), taps_of(2, g)
         decay = [per_mode(dec_n, g, m) for m in range(modes)]
         behind = range(SUB - taps + 1, SUB)
@@ -224,24 +215,59 @@
         for m in range(modes):
             e_loc[pl.ds(g * SUB * modes + m, SUB, stride=modes), :] = state[m]
 
-    rims[0].wait_recv()
-    rims[1].wait_recv()
-    relayout_rim(rim_k, xk)
-    relayout_rim(rim_v, xv)
-
-    @pl.loop(0, groups)
+    side = 4
+
+    def nth(i, j):
+        near = lambda n: (n * (n + 1) // 2) % side
+        y = lax.rem(spot // side + near(i), side)
+        x = lax.rem(spot + near(j), side)
+        return y * side + x
+
+    def nth_of(n):
+        return nth(n // side, lax.rem(n, side))
+
+    @pl.loop(0, groups // 2)
     def _(g):
-        k_taps, v_taps = taps_of(1, g), taps_of(2, g)
-        decay = [per_mode(dec_n, g, m) for m in range(modes)]
-        behind = range(SUB - taps + 1, SUB)
-        _, _, state = block_of_z(
-            1, g, [token(xk, 0, g, s) for s in behind], [token(xv, 0, g, s) for s in behind],
-            [zero] * modes, k_taps, v_taps, decay,
-        )
-        for m in range(modes):
-            rest = jnp.exp(per_mode(rate_n, g, m) * float(SUB - tok))
-            here = pl.ds(g * SUB * modes + m, SUB, stride=modes)
-            e_loc[here, :] = e_loc[here, :] + rest * state[m]
+        end_states(g)
+
+    owned = chans // PLANE
+    for owner in range(PLANE):
+        cols = slice(owner * owned, (owner + 1) * owned)
+        edge[owner, 0] = k_in[tok - SUB : tok, cols]
+        edge[owner, 1] = v_in[tok - SUB : tok, cols]
+        edge[owner, 2] = k_in[0:SUB, cols]
+        edge[owner, 3] = v_in[0:SUB, cols]
+
+    crossing = ((spot + 1) // PLANE) * ((2 * planes - 3 - zed) // (planes - 1))
+    crosses = crossing > 0
+    pl.semaphore_wait(barrier, PLANE - 1 + planes - 1 + 2 + PLANE * crossing)
+
+    def edge_copy(owner, slot, plane, kind):
+        return pltpu.make_async_remote_copy(
+            src_ref=edge.at[owner], dst_ref=edges.at[slot],
+            send_sem=edge_send.at[kind, owner], recv_sem=edge_recv.at[slot],
+            device_id=(plane * PLANE + owner, core), device_id_type=MESH,
+        )
+
+    @pl.loop(1, PLANE)
+    def _(step):
+        edge_copy(nth_of(PLANE - step), spot, zed, 0).start()
+
+    @pl.when(crosses)
+    def _():
+        @pl.loop(0, PLANE)
+        def _(owner):
+            edge_copy(owner, PLANE, zed + 1, 1).start()
+
+    edges[spot] = edge[spot]
+
+    @pl.when(zed == 0)
+    def _():
+        edges[PLANE] = jnp.zeros_like(edges[PLANE])
+
+    @pl.loop(groups // 2, groups)
+    def _(g):
+        end_states(g)
 
     def round_1(other):
         return pltpu.make_async_remote_copy(
@@ -257,20 +283,20 @@
             device_id=(zed * PLANE + other, core), device_id_type=MESH,
         )
 
-    side = 4
-
-    def nth(i, j):
-        near = lambda n: (n * (n + 1) // 2) % side
-        y = lax.rem(spot // side + near(i), side)
-        x = lax.rem(spot + near(j), side)
-        return y * side + x
-
-    def nth_of(n):
-        return nth(n // side, lax.rem(n, side))
-
     @pl.loop(1, PLANE)
     def _(step):
         round_1(nth_of(PLANE - step)).start()
+
+    def rim_copy(index, src, dst):
+        return pltpu.make_async_remote_copy(
+            src_ref=src.at[pl.ds(tok - SUB, SUB)], dst_ref=dst,
+            send_sem=rim_send.at[index], recv_sem=rim_recv.at[index],
+            device_id=(after, core), device_id_type=MESH,
+        )
+
+    rims = [rim_copy(0, k_hbm, rim_k), rim_copy(1, v_hbm, rim_v), rim_copy(2, q_hbm, rim_q)]
+    for copy in rims:
+        copy.start()
 
     e_buf[spot] = at(e_loc, spot * part, part)[...]
 
@@ -294,14 +320,67 @@
         load(0, q_hbm, q_in, g).wait()
         relayout(q_in, xq, g)
 
-    rims[2].wait_recv()
-    relayout_rim(rim_q, xq)
+    rising = (lax.broadcasted_iota(jnp.int32, (SUB, LANES), 0) + 1).astype(F32)
+
+    @pl.loop(0, tiles)
+    def _(t):
+        for m in range(modes):
+            rate = rate_n[pl.ds(t * modes + m, 1), :]
+            coef = coef_n[pl.ds(t * modes + m, 1), :]
+            here = pl.ds(pl.multiple_of((t * modes + m) * SUB, SUB), SUB)
+            weights[here, :] = coef * jnp.exp(-rate * rising)
+        whole = pl.ds(pl.multiple_of(t * modes, SUB), modes)
+        dec8_n[whole, :] = jnp.exp(rate_n[whole, :] * float(-SUB))
+
+    per = tiles // PLANE
+    my_rate = at(rate_n, spot * part, part)[...]
+    for i in range(SUB):
+        source = pl.multiple_of((spot * per + i % per) * SUB, SUB)
+        dec_own[i * SUB : (i + 1) * SUB, :] = dec_n[pl.ds(source, SUB), :]
+        for a in (1, 2):
+            taps_own[a - 1, i * SUB : (i + 1) * SUB, :] = taps_t[a, pl.ds(source, SUB), :]
+    own_decay = [dec_own[pl.ds(m, SUB, stride=modes), :] for m in range(modes)]
+    own_taps = [[taps_own[a, pl.ds(j, SUB, stride=SUB), :] for j in range(taps)] for a in range(2)]
 
     @pl.loop(1, PLANE)
     def _(step):
+        source = lax.rem(spot + step, PLANE)
+        edge_copy(source, source, zed, 0).wait_recv()
+
+    @pl.when(zed > 0)
+    def _():
+        edge_copy(spot, PLANE, zed, 1).wait_recv()
+
+    for j in range(PLANE):
+        for a, dst in ((0, ek), (1, ev)):
+            past = edges[(j + PLANE) % (PLANE + 1), a].astype(F32)
+            here = edges[j, a + 2].astype(F32)
+            for i in range(per):
+                tile = j * per + i
+                dst[row_of(0, tile) : row_of(0, tile) + SUB, :] = past[:, i * LANES : (i + 1) * LANES]
+                dst[row_of(1, tile) : row_of(1, tile) + SUB, :] = here[:, i * LANES : (i + 1) * LANES]
+
+    for g in range(groups):
+        shard = zed * PLANE + (lax.broadcasted_iota(jnp.int32, (SUB, LANES), 0) + g * SUB) // per
+        begin = shard * tok
+        latest = jnp.full((SUB, LANES), -1, jnp.int32)
+        for end in ends:
+            latest = jnp.maximum(latest, jnp.where(end <= begin + (tok - 1), end, -1))
+        window = [[token(x, 0, g, s) for s in range(SUB - taps + 1, SUB)] for x in (ek, ev)]
+        state = [zero] * modes
+        for s in range(SUB):
+            window[0].append(token(ek, 1, g, s))
+            window[1].append(token(ev, 1, g, s))
+            z = fir(window[0][-taps:], own_taps[0]) * fir(window[1][-taps:], own_taps[1])
+            z = jnp.where(begin + s >= latest, z, 0.0)
+            state = [d * old + z for d, old in zip(own_decay, state)]
+        for m in range(modes):
+            e_first[pl.ds(g * SUB * modes + m, SUB, stride=modes), :] = state[m]
+
+    @pl.loop(1, PLANE)
+    def _(step):
         arrival_1(lax.rem(spot + step, PLANE)).wait_recv()
 
-    my_rate = at(rate_n, spot * part, part)[...]
     span = jnp.exp(my_rate * float(-tok))
     spot_rows = lax.broadcasted_iota(jnp.int32, (PLANE, LANES), 0) + zed * PLANE
     plane_rows = lax.broadcasted_iota(jnp.int32, (SUB, LANES), 0)
@@ -311,13 +390,14 @@
         open_here = jnp.where(spot_rows == end // tok, 0.0, open_here)
         open_plane = jnp.where(plane_rows == end // (tok * PLANE), 0.0, open_plane)
 
+    rest = jnp.exp(my_rate * float(SUB - tok))
     state = jnp.zeros_like(span)
     reach = jnp.ones_like(span)
     for other in range(PLANE):
         pre_buf[other] = state
         reach_buf[other] = reach
         factor = span * open_here[other : other + 1]
-        state = factor * state + e_buf[other]
+        state = factor * state + e_buf[other] + rest * e_first[other * part : (other + 1) * part, :]
         reach = factor * reach
     total_buf[...] = state
 
@@ -331,6 +411,20 @@
     @pl.loop(zed + 1, planes)
     def _(there):
         round_2(there, zed).start()
+
+    for copy in rims:
+        copy.wait_recv()
+    relayout_rim(rim_k, xk)
+    relayout_rim(rim_v, xv)
+    relayout_rim(rim_q, xq)
+
+    @pl.loop(0, groups)
+    def _(g):
+        behind = range(SUB - taps + 1, SUB)
+        block_of_z(
+            1, g, [token(xk, 0, g, s) for s in behind], [token(xv, 0, g, s) for s in behind],
+            [], taps_of(1, g), taps_of(2, g), [],
+        )
 
     def inner(g):
         q_taps = taps_of(0, g)
@@ -389,18 +483,6 @@
     def _(g):
         inner(g)
 
-    rising = (lax.broadcasted_iota(jnp.int32, (SUB, LANES), 0) + 1).astype(F32)
-
-    @pl.loop(0, tiles)
-    def _(t):
-        for m in range(modes):
-            rate = rate_n[pl.ds(t * modes + m, 1), :]
-            coef = coef_n[pl.ds(t * modes + m, 1), :]
-            here = pl.ds(pl.multiple_of((t * modes + m) * SUB, SUB), SUB)
-            weights[here, :] = coef * jnp.exp(-rate * rising)
-        whole = pl.ds(pl.multiple_of(t * modes, SUB), modes)
-        dec8_n[whole, :] = jnp.exp(rate_n[whole, :] * float(-SUB))
-
     for g in range(groups):
         load(3, r_hbm, r_in, g).wait()
 
@@ -415,7 +497,6 @@
 
     sq_loc[...] = jnp.zeros_like(sq_loc)
 
-    per = tiles // PLANE
 
     def tree(terms):
         while len(terms) > 1:
@@ -469,6 +550,13 @@
         other = lax.rem(spot + step, PLANE)
         round_1(other).wait_send()
         round_3(other, spot).wait_send()
+        edge_copy(other, spot, zed, 0).wait_send()
+
+    @pl.when(crosses)
+    def _():
+        @pl.loop(0, PLANE)
+        def _(owner):
+            edge_copy(owner, PLANE, zed + 1, 1).wait_send()
 
     @pl.loop(zed + 1, planes)
     def _(there):
@@ -485,16 +573,16 @@
     groups = chans // wide
     copies = [pltpu.make_async_copy(stream_ref, stream_hbm, sem.at[groups])]
     copies[0].start()
+    scales = [scale_ref[pair * 2 * SUB : (pair + 1) * 2 * SUB, :] for pair in range(tok // (2 * SUB))]
     for g in range(groups):
-        for t in range(g * SUB, (g + 1) * SUB):
-            cols = slice(t * LANES, (t + 1) * LANES)
-            gain = gain_ref[t : t + 1, :]
-
-            @pl.loop(0, tok // (2 * SUB))
-            def _(pair):
-                both = pl.ds(pl.multiple_of(pair * 2 * SUB, 2 * SUB), 2 * SUB)
+        @pl.loop(g * SUB, (g + 1) * SUB)
+        def _(t):
+            cols = pl.ds(pl.multiple_of(t * LANES, LANES), LANES)
+            gain = gain_ref[pl.ds(t, 1), :]
+            for pair, scale in enumerate(scales):
+                both = slice(pair * 2 * SUB, (pair + 1) * 2 * SUB)
                 x = stream_ref[both, cols].astype(F32)
-                normed[both, cols] = (x * scale_ref[both, :] * gain).astype(jnp.bfloat16)
+                normed[both, cols] = (x * scale * gain).astype(jnp.bfloat16)
 
         part = slice(g * wide, (g + 1) * wide)
         copy = pltpu.make_async_copy(normed.at[:, part], normed_hbm.at[:, part], sem.at[g])
@@ -534,6 +622,9 @@
             vmem((3, taps, chans), F32), vmem((modes, chans), F32), vmem((modes, chans), F32),
             pltpu.SMEM((segs,), jnp.int32),
             vmem((SUB, chans), bf16), vmem((SUB, chans), bf16), vmem((SUB, chans), bf16),
+            vmem((PLANE, 4, SUB, chans // PLANE), bf16), vmem((PLANE + 1, 4, SUB, chans // PLANE), bf16),
+            vmem((2 * tiles * SUB, LANES), F32), vmem((2 * tiles * SUB, LANES), F32),
+            vmem((tiles * modes, LANES), F32), vmem((SUB * modes, LANES), F32), vmem((2, SUB * SUB, LANES), F32),
             vmem(((blocks + 1) * tiles * SUB, LANES), F32),
             vmem(((blocks + 1) * tiles * SUB, LANES), F32),
             vmem(((blocks + 1) * tiles * SUB, LANES), F32),
@@ -548,7 +639,7 @@
             vmem((PLANE, part, LANES), F32), vmem((PLANE, part, LANES), F32), vmem((PLANE, part, LANES), F32),
             vmem((part, LANES), F32), vmem((planes, part, LANES), F32), vmem((PLANE, part, LANES), F32),
             vmem((tok, LANES), F32), vmem((tok, LANES), F32),
-            sem((4, groups)), sem((5,)), sem((3,)), sem((3,)),
+            sem((4, groups)), sem((5,)), sem((3,)), sem((3,)), sem((2, PLANE)), sem((PLANE + 1,)),
             sem((PLANE,)), sem((PLANE,)), sem((planes,)), sem((planes,)), sem((PLANE,)), sem((PLANE,)),
             sem, sem,
         ],

time: 37.1 us -> 36.4 us (0.981)
  Pallas kernels: 36.3 us -> 35.7 us
    pallas_call x1, Pallas kernels: 2.77 us -> 1.35 us  [body(): pl.pallas_call(functools.partial(finish, tok, chans), out_shape=(jax.Shap...]
    pallas_call x1, Pallas kernels: 33.5 us -> 34.3 us  [body(): pl.pallas_call(functools.partial(kernel, dims), out_shape=(jax.ShapeDtype...]
where the time goes in v3:
time: 36.4 us; the launch traced here: 36.3 us
  Pallas kernels  35.7 us (98%)
  between operations  0.64 us (2%)
    pallas_call x1, Pallas kernels, body(): pl.pallas_call(functools.partial(kernel, dims), out_shape=(jax.ShapeDtype...  34.3 us
    pallas_call x1, Pallas kernels, body(): pl.pallas_call(functools.partial(finish, tok, chans), out_shape=(jax.Shap...  1.35 us

profile of v3, /device:TPU:1, one launch (start us, length us, event | category | flops | bytes accessed | tf_op | source)
XLA Modules:
  0.0 36.3 jit_solution(11304247874754531873)
XLA Ops:
  0.6 34.3 %hyena.1 = (bf16[128,4096]{1,0:T(8,128)(2,1)S(1)}, f32[128,128]{1,0:T(8,128)S(1)}, f32[32,128]{1,0:T(8,128)S(1)}) custom-call(bf16[128,4096]{1,0:T(8,128)(2,1)} %q_hbm.1, bf16[128,4096]{1,0:T(8,128)(2,1)} %k_hbm.1, bf16[128,4096]{1,0:T(8,128)(2,1)} %v_hbm.1, bf16[128,4096]{1,0:T(8,128)(2,1)} %r_hbm.1, f32[3,7,4096]{2,1,0:T(8,128)} %sf_hbm.1, ...), custom_call_target="tpu_custom_call" | custom-call | tf_op jit(solution)/shard_map/hyena/pallas_call | solution.py:611
  35.0 1.4 %finish.1 = (bf16[128,4096]{1,0:T(8,128)(2,1)}, bf16[128,4096]{1,0:T(8,128)(2,1)}) custom-call(bf16[128,4096]{1,0:T(8,128)(2,1)S(1)} %get-tuple-element.5.stream_ref, f32[128,128]{1,0:T(8,128)S(1)} %get-tuple-element.6.scale_ref, f32[32,128]{1,0:T(8,128)S(1)} %get-tuple-element.7.gain_ref), custom_call_target="tpu_custom_call" | custom-call | tf_op jit(solution)/shard_map/finish/pallas_call | solution.py:653

commit v4 on v3

--- a/solution.py
+++ b/solution.py
@@ -18,7 +18,7 @@
     q_hbm, k_hbm, v_hbm, r_hbm, sf_hbm, residue_hbm, rate_hbm, gain_hbm, seg_hbm,
     stream_ref, scale_ref, gain_in,
     q_in, k_in, v_in, r_in, sf_in, residue_in, rate_in, seg_ref,
-    rim_q, rim_k, rim_v, edge, edges, ek, ev, e_first, dec_own, taps_own,
+    rim_q, rim_k, rim_v, edge, edges, ek, ev, e_first, head_n, dec_own, taps_own,
     xq, xk, xv, zs, conv_std, qs_std,
     taps_t, rate_n, coef_n, dec_n, weights, dec8_n,
     keep_m, last_m, carry_m,
@@ -96,13 +96,16 @@
         ends.append(running)
     big = jnp.int32(1 << 30)
     low = big
+    low8 = big
     high = jnp.int32(-1)
     for end in ends:
         low = jnp.minimum(low, jnp.where(end >= first, end, big))
+        low8 = jnp.minimum(low8, jnp.where(end >= first + SUB, end, big))
         high = jnp.maximum(high, jnp.where(end <= first + tok - 1, end, -1))
     rows = lax.broadcasted_iota(jnp.int32, (tok, LANES), 0) + first
     last_m[...] = jnp.where(rows >= high, 1.0, 0.0)
-    carry_m[...] = jnp.where(rows < low, 1.0, 0.0)
+    carry_m[...] = jnp.where(rows < low8, 1.0, 0.0)
+    carry_m[:SUB, :] = jnp.where(rows[:SUB] < low, 1.0, 0.0)
 
     params[0].wait()
     for t in range(tiles):
@@ -331,6 +334,57 @@
             weights[here, :] = coef * jnp.exp(-rate * rising)
         whole = pl.ds(pl.multiple_of(t * modes, SUB), modes)
         dec8_n[whole, :] = jnp.exp(rate_n[whole, :] * float(-SUB))
+
+    def tree(terms):
+        while len(terms) > 1:
+            terms = [a + b for a, b in zip(terms[::2], terms[1::2])]
+        return terms[0]
+
+    def conv_block(block, g, q_win, state, q_taps, decay, coef, z_of):
+        q_win, state = list(q_win), list(state)
+        for s in range(SUB):
+            q_win.append(token(xq, block, g, s))
+            qs = fir(q_win[-taps:], q_taps)
+            t = (block - 1) * SUB + s
+            z = z_of(t, s)
+            keep = keep_m[pl.ds(t, 1), :]
+            state = [(d * keep) * old + z for d, old in zip(decay, state)]
+            out = tree([c * part for c, part in zip(coef, state)])
+            there = pl.ds(row_of(block - 1, g * SUB) + s, SUB, stride=SUB)
+            conv_std[there, :] = out * qs
+            qs_std[there, :] = qs * carry_m[pl.ds(t, 1), :]
+        return q_win[1 - taps :], state
+
+    behind = range(SUB - taps + 1, SUB)
+
+    def inner(g):
+        q_taps = taps_of(0, g)
+        decay = [per_mode(dec_n, g, m) for m in range(modes)]
+        coef = [per_mode(coef_n, g, m) for m in range(modes)]
+
+        def step(block, carried):
+            return conv_block(block, g, *carried, q_taps, decay, coef, lambda t, s: zs[z_rows(t, g), :])
+
+        lax.fori_loop(2, blocks + 1, step, ([token(xq, 1, g, s) for s in behind], [zero] * modes))
+
+    def head(g):
+        windows = [[token(x, 0, g, s) for s in behind] for x in (xk, xv)]
+        weight = [taps_of(1, g), taps_of(2, g)]
+
+        def z_of(t, s):
+            for window, x in zip(windows, (xk, xv)):
+                window.append(token(x, 1, g, s))
+            return fir(windows[0][-taps:], weight[0]) * fir(windows[1][-taps:], weight[1])
+
+        decay = [per_mode(dec_n, g, m) for m in range(modes)]
+        coef = [per_mode(coef_n, g, m) for m in range(modes)]
+        _, state = conv_block(
+            1, g, [token(xq, 0, g, s) for s in behind], [zero] * modes, taps_of(0, g), decay, coef, z_of
+        )
+        for m in range(modes):
+            head_n[pl.ds(g * SUB * modes + m, SUB, stride=modes), :] = state[m]
+
+    inner(0)
 
     per = tiles // PLANE
     my_rate = at(rate_n, spot * part, part)[...]
@@ -412,47 +466,7 @@
     def _(there):
         round_2(there, zed).start()
 
-    for copy in rims:
-        copy.wait_recv()
-    relayout_rim(rim_k, xk)
-    relayout_rim(rim_v, xv)
-    relayout_rim(rim_q, xq)
-
-    @pl.loop(0, groups)
-    def _(g):
-        behind = range(SUB - taps + 1, SUB)
-        block_of_z(
-            1, g, [token(xk, 0, g, s) for s in behind], [token(xv, 0, g, s) for s in behind],
-            [], taps_of(1, g), taps_of(2, g), [],
-        )
-
-    def inner(g):
-        q_taps = taps_of(0, g)
-        decay = [per_mode(dec_n, g, m) for m in range(modes)]
-        coef = [per_mode(coef_n, g, m) for m in range(modes)]
-        behind = range(SUB - taps + 1, SUB)
-
-        def step(block, carried):
-            q_win, state = list(carried[0]), list(carried[1])
-            for s in range(SUB):
-                q_win.append(token(xq, block, g, s))
-                qs = fir(q_win[-taps:], q_taps)
-                t = (block - 1) * SUB + s
-                z = zs[z_rows(t, g), :]
-                keep = keep_m[pl.ds(t, 1), :]
-                state = [(d * keep) * old + z for d, old in zip(decay, state)]
-                out = coef[0] * state[0]
-                for m in range(1, modes):
-                    out = out + coef[m] * state[m]
-                there = pl.ds(row_of(block - 1, g * SUB) + s, SUB, stride=SUB)
-                conv_std[there, :] = out * qs
-                qs_std[there, :] = qs * carry_m[pl.ds(t, 1), :]
-            return q_win[1 - taps :], state
-
-        start = ([token(xq, 0, g, s) for s in behind], [zero] * modes)
-        lax.fori_loop(1, blocks + 1, step, start)
-
-    @pl.loop(0, groups // 2)
+    @pl.loop(1, groups - 1)
     def _(g):
         inner(g)
 
@@ -479,9 +493,17 @@
 
     inc_buf[spot] = pre_buf[spot] + reach_buf[spot] * state
 
-    @pl.loop(groups // 2, groups)
+    inner(groups - 1)
+
+    for copy in rims:
+        copy.wait_recv()
+    relayout_rim(rim_k, xk)
+    relayout_rim(rim_v, xv)
+    relayout_rim(rim_q, xq)
+
+    @pl.loop(0, groups)
     def _(g):
-        inner(g)
+        head(g)
 
     for g in range(groups):
         load(3, r_hbm, r_in, g).wait()
@@ -498,24 +520,26 @@
     sq_loc[...] = jnp.zeros_like(sq_loc)
 
 
-    def tree(terms):
-        while len(terms) > 1:
-            terms = [a + b for a, b in zip(terms[::2], terms[1::2])]
-        return terms[0]
-
     def tile_of(slot, local):
         t = slot * per + local
-        value, decay = [], []
+        whole = pl.ds(pl.multiple_of(t * modes, SUB), modes)
+        incoming = inc_buf[slot, local * modes : (local + 1) * modes, :]
+        at_8 = dec8_n[whole, :] * carry_m[SUB - 1 : SUB, :] * incoming + head_n[whole, :]
+        value, later, decay = [], [], []
         for m in range(modes):
             here = pl.ds(pl.multiple_of((t * modes + m) * SUB, SUB), SUB)
-            value.append(weights[here, :] * inc_buf[slot, pl.ds(local * modes + m, 1), :])
+            weight = weights[here, :]
+            value.append(weight * incoming[m : m + 1])
+            later.append(weight * at_8[m : m + 1])
             decay.append(jnp.broadcast_to(dec8_n[pl.ds(t * modes + m, 1), :], (SUB, LANES)))
         cols = pl.ds(pl.multiple_of(t * LANES, LANES), LANES)
         for pair in range(pairs):
             halves = []
             for block in (2 * pair, 2 * pair + 1):
                 carried = tree(value)
-                if block < blocks - 1:
+                if block == 0:
+                    value = later
+                elif block < blocks - 1:
                     value = [v * d for v, d in zip(value, decay)]
                 here = pl.ds(pl.multiple_of(row_of(block, t), SUB), SUB)
                 halves.append(conv_std[here, :] + qs_std[here, :] * carried)
@@ -624,7 +648,8 @@
             vmem((SUB, chans), bf16), vmem((SUB, chans), bf16), vmem((SUB, chans), bf16),
             vmem((PLANE, 4, SUB, chans // PLANE), bf16), vmem((PLANE + 1, 4, SUB, chans // PLANE), bf16),
             vmem((2 * tiles * SUB, LANES), F32), vmem((2 * tiles * SUB, LANES), F32),
-            vmem((tiles * modes, LANES), F32), vmem((SUB * modes, LANES), F32), vmem((2, SUB * SUB, LANES), F32),
+            vmem((tiles * modes, LANES), F32), vmem((tiles * modes, LANES), F32),
+            vmem((SUB * modes, LANES), F32), vmem((2, SUB * SUB, LANES), F32),
             vmem(((blocks + 1) * tiles * SUB, LANES), F32),
             vmem(((blocks + 1) * tiles * SUB, LANES), F32),
             vmem(((blocks + 1) * tiles * SUB, LANES), F32),

time: 36.4 us -> 32.4 us (0.89)
  Pallas kernels: 35.7 us -> 31.7 us
    pallas_call x1, Pallas kernels: 34.3 us -> 30.3 us  [body(): pl.pallas_call(functools.partial(kernel, dims), out_shape=(jax.ShapeDtype...]
where the time goes in v4:
time: 32.4 us; the launch traced here: 32.3 us
  Pallas kernels  31.7 us (98%)
  between operations  0.64 us (2%)
    pallas_call x1, Pallas kernels, body(): pl.pallas_call(functools.partial(kernel, dims), out_shape=(jax.ShapeDtype...  30.3 us
    pallas_call x1, Pallas kernels, body(): pl.pallas_call(functools.partial(finish, tok, chans), out_shape=(jax.Shap...  1.35 us

profile of v4, /device:TPU:1, one launch (start us, length us, event | category | flops | bytes accessed | tf_op | source)
XLA Modules:
  0.0 32.3 jit_solution(6408155308855684350)
XLA Ops:
  0.6 30.3 %hyena.1 = (bf16[128,4096]{1,0:T(8,128)(2,1)S(1)}, f32[128,128]{1,0:T(8,128)S(1)}, f32[32,128]{1,0:T(8,128)S(1)}) custom-call(bf16[128,4096]{1,0:T(8,128)(2,1)} %q_hbm.1, bf16[128,4096]{1,0:T(8,128)(2,1)} %k_hbm.1, bf16[128,4096]{1,0:T(8,128)(2,1)} %v_hbm.1, bf16[128,4096]{1,0:T(8,128)(2,1)} %r_hbm.1, f32[3,7,4096]{2,1,0:T(8,128)} %sf_hbm.1, ...), custom_call_target="tpu_custom_call" | custom-call | tf_op jit(solution)/shard_map/hyena/pallas_call | solution.py:635
  31.0 1.4 %finish.1 = (bf16[128,4096]{1,0:T(8,128)(2,1)}, bf16[128,4096]{1,0:T(8,128)(2,1)}) custom-call(bf16[128,4096]{1,0:T(8,128)(2,1)S(1)} %get-tuple-element.5.stream_ref, f32[128,128]{1,0:T(8,128)S(1)} %get-tuple-element.6.scale_ref, f32[32,128]{1,0:T(8,128)S(1)} %get-tuple-element.7.gain_ref), custom_call_target="tpu_custom_call" | custom-call | tf_op jit(solution)/shard_map/finish/pallas_call | solution.py:678

commit v5 on v4

--- a/solution.py
+++ b/solution.py
@@ -59,13 +59,6 @@
     for g in range(groups):
         load(1, k_hbm, k_in, g).start()
         load(2, v_hbm, v_in, g).start()
-    for index in (2, 3):
-        params[index].start()
-    for g in range(groups):
-        load(0, q_hbm, q_in, g).start()
-    for g in range(groups):
-        load(3, r_hbm, r_in, g).start()
-
     barrier = pltpu.get_barrier_semaphore()
 
     @pl.loop(1, PLANE)
@@ -179,10 +172,6 @@
         relayout_tile(k_in, xk, 0, 0, j)
         relayout_tile(v_in, xv, 0, 0, j)
 
-    for g in range(groups - 1):
-        load(1, k_hbm, k_in, g + 1).wait()
-        load(2, v_hbm, v_in, g + 1).wait()
-
     def end_states(g):
         k_taps, v_taps = taps_of(1, g), taps_of(2, g)
         decay = [per_mode(dec_n, g, m) for m in range(modes)]
@@ -231,7 +220,19 @@
 
     @pl.loop(0, groups // 2)
     def _(g):
+        load(1, k_hbm, k_in, g + 1).wait()
+        load(2, v_hbm, v_in, g + 1).wait()
         end_states(g)
+
+    for g in range(groups // 2 + 1, groups):
+        load(1, k_hbm, k_in, g).wait()
+        load(2, v_hbm, v_in, g).wait()
+    for index in (2, 3):
+        params[index].start()
+    for g in range(groups):
+        load(0, q_hbm, q_in, g).start()
+    for g in range(groups):
+        load(3, r_hbm, r_in, g).start()
 
     owned = chans // PLANE
     for owner in range(PLANE):
@@ -298,9 +299,6 @@
         )
 
     rims = [rim_copy(0, k_hbm, rim_k), rim_copy(1, v_hbm, rim_v), rim_copy(2, q_hbm, rim_q)]
-    for copy in rims:
-        copy.start()
-
     e_buf[spot] = at(e_loc, spot * part, part)[...]
 
     begins = rows == 0
@@ -465,6 +463,9 @@
     @pl.loop(zed + 1, planes)
     def _(there):
         round_2(there, zed).start()
+
+    for copy in rims:
+        copy.start()
 
     @pl.loop(1, groups - 1)
     def _(g):

time: 32.4 us -> 36.7 us (1.13)
  Pallas kernels: 31.7 us -> 35.9 us
    pallas_call x1, Pallas kernels: 30.3 us -> 34.6 us  [body(): pl.pallas_call(functools.partial(kernel, dims), out_shape=(jax.ShapeDtype...]
where the time goes in v5:
time: 36.7 us; the launch traced here: 36.6 us
  Pallas kernels  35.9 us (98%)
  between operations  0.64 us (2%)
    pallas_call x1, Pallas kernels, body(): pl.pallas_call(functools.partial(kernel, dims), out_shape=(jax.ShapeDtype...  34.6 us
    pallas_call x1, Pallas kernels, body(): pl.pallas_call(functools.partial(finish, tok, chans), out_shape=(jax.Shap...  1.35 us

profile of v5, /device:TPU:1, one launch (start us, length us, event | category | flops | bytes accessed | tf_op | source)
XLA Modules:
  0.0 36.6 jit_solution(8550858957723375680)
XLA Ops:
  0.6 34.6 %hyena.1 = (bf16[128,4096]{1,0:T(8,128)(2,1)S(1)}, f32[128,128]{1,0:T(8,128)S(1)}, f32[32,128]{1,0:T(8,128)S(1)}) custom-call(bf16[128,4096]{1,0:T(8,128)(2,1)} %q_hbm.1, bf16[128,4096]{1,0:T(8,128)(2,1)} %k_hbm.1, bf16[128,4096]{1,0:T(8,128)(2,1)} %v_hbm.1, bf16[128,4096]{1,0:T(8,128)(2,1)} %r_hbm.1, f32[3,7,4096]{2,1,0:T(8,128)} %sf_hbm.1, ...), custom_call_target="tpu_custom_call" | custom-call | tf_op jit(solution)/shard_map/hyena/pallas_call | solution.py:636
  35.2 1.4 %finish.1 = (bf16[128,4096]{1,0:T(8,128)(2,1)}, bf16[128,4096]{1,0:T(8,128)(2,1)}) custom-call(bf16[128,4096]{1,0:T(8,128)(2,1)S(1)} %get-tuple-element.5.stream_ref, f32[128,128]{1,0:T(8,128)S(1)} %get-tuple-element.6.scale_ref, f32[32,128]{1,0:T(8,128)S(1)} %get-tuple-element.7.gain_ref), custom_call_target="tpu_custom_call" | custom-call | tf_op jit(solution)/shard_map/finish/pallas_call | solution.py:679

commit v6 on v5

--- a/solution.py
+++ b/solution.py
@@ -42,6 +42,37 @@
     def at(ref, start, size):
         return ref.at[pl.ds(pl.multiple_of(start, SUB), size)]
 
+    side = 4
+
+    def nth(i, j):
+        near = lambda n: (n * (n + 1) // 2) % side
+        y = lax.rem(spot // side + near(i), side)
+        x = lax.rem(spot + near(j), side)
+        return y * side + x
+
+    def nth_of(n):
+        return nth(n // side, lax.rem(n, side))
+
+    barrier = pltpu.get_barrier_semaphore()
+
+    @pl.loop(1, PLANE)
+    def _(step):
+        other = zed * PLANE + nth_of(PLANE - step)
+        pl.semaphore_signal(barrier, inc=1, device_id=(other, core), device_id_type=MESH)
+
+    @pl.loop(1, planes)
+    def _(step):
+        other = lax.rem(zed + step, planes) * PLANE + spot
+        pl.semaphore_signal(barrier, inc=1, device_id=(other, core), device_id_type=MESH)
+
+    @pl.when(zed > 0)
+    def _():
+        last = (zed - 1) * PLANE + PLANE - 1
+        pl.semaphore_signal(barrier, inc=1, device_id=(last, core), device_id_type=MESH)
+
+    pl.semaphore_signal(barrier, inc=1, device_id=(before, core), device_id_type=MESH)
+    pl.semaphore_signal(barrier, inc=1, device_id=(me, 1 - core), device_id_type=MESH)
+
     params = [
         pltpu.make_async_copy(rate_hbm, rate_in, param_sem.at[0]),
         pltpu.make_async_copy(sf_hbm, sf_in, param_sem.at[1]),
@@ -59,26 +90,6 @@
     for g in range(groups):
         load(1, k_hbm, k_in, g).start()
         load(2, v_hbm, v_in, g).start()
-    barrier = pltpu.get_barrier_semaphore()
-
-    @pl.loop(1, PLANE)
-    def _(step):
-        other = zed * PLANE + lax.rem(spot + step, PLANE)
-        pl.semaphore_signal(barrier, inc=1, device_id=(other, core), device_id_type=MESH)
-
-    @pl.loop(1, planes)
-    def _(step):
-        other = lax.rem(zed + step, planes) * PLANE + spot
-        pl.semaphore_signal(barrier, inc=1, device_id=(other, core), device_id_type=MESH)
-
-    @pl.when(zed > 0)
-    def _():
-        last = (zed - 1) * PLANE + PLANE - 1
-        pl.semaphore_signal(barrier, inc=1, device_id=(last, core), device_id_type=MESH)
-
-    pl.semaphore_signal(barrier, inc=1, device_id=(before, core), device_id_type=MESH)
-    pl.semaphore_signal(barrier, inc=1, device_id=(me, 1 - core), device_id_type=MESH)
-
     params[4].wait()
     first = me * tok
     ends = []
@@ -207,17 +218,6 @@
         for m in range(modes):
             e_loc[pl.ds(g * SUB * modes + m, SUB, stride=modes), :] = state[m]
 
-    side = 4
-
-    def nth(i, j):
-        near = lambda n: (n * (n + 1) // 2) % side
-        y = lax.rem(spot // side + near(i), side)
-        x = lax.rem(spot + near(j), side)
-        return y * side + x
-
-    def nth_of(n):
-        return nth(n // side, lax.rem(n, side))
-
     @pl.loop(0, groups // 2)
     def _(g):
         load(1, k_hbm, k_in, g + 1).wait()
@@ -299,6 +299,9 @@
         )
 
     rims = [rim_copy(0, k_hbm, rim_k), rim_copy(1, v_hbm, rim_v), rim_copy(2, q_hbm, rim_q)]
+    for copy in rims:
+        copy.start()
+
     e_buf[spot] = at(e_loc, spot * part, part)[...]
 
     begins = rows == 0
@@ -464,9 +467,6 @@
     def _(there):
         round_2(there, zed).start()
 
-    for copy in rims:
-        copy.start()
-
     @pl.loop(1, groups - 1)
     def _(g):
         inner(g)
@@ -495,6 +495,22 @@
     inc_buf[spot] = pre_buf[spot] + reach_buf[spot] * state
 
     inner(groups - 1)
+
+    @pl.loop(1, PLANE)
+    def _(step):
+        other = lax.rem(spot + step, PLANE)
+        round_1(other).wait_send()
+        edge_copy(other, spot, zed, 0).wait_send()
+
+    @pl.when(crosses)
+    def _():
+        @pl.loop(0, PLANE)
+        def _(owner):
+            edge_copy(owner, PLANE, zed + 1, 1).wait_send()
+
+    @pl.loop(zed + 1, planes)
+    def _(there):
+        round_2(there, zed).wait_send()
 
     for copy in rims:
         copy.wait_recv()
@@ -573,19 +589,7 @@
     @pl.loop(1, PLANE)
     def _(step):
         other = lax.rem(spot + step, PLANE)
-        round_1(other).wait_send()
         round_3(other, spot).wait_send()
-        edge_copy(other, spot, zed, 0).wait_send()
-
-    @pl.when(crosses)
-    def _():
-        @pl.loop(0, PLANE)
-        def _(owner):
-            edge_copy(owner, PLANE, zed + 1, 1).wait_send()
-
-    @pl.loop(zed + 1, planes)
-    def _(there):
-        round_2(there, zed).wait_send()
 
     swap.wait()
     total = jnp.sum(sq_loc[...] + sq_far[...], axis=1, keepdims=True)

time: 36.7 us -> 32.6 us (0.89)
  Pallas kernels: 35.9 us -> 31.9 us
    pallas_call x1, Pallas kernels: 34.6 us -> 30.5 us  [body(): pl.pallas_call(functools.partial(kernel, dims), out_shape=(jax.ShapeDtype...]
where the time goes in v6:
time: 32.6 us; the launch traced here: 32.5 us
  Pallas kernels  31.9 us (98%)
  between operations  0.64 us (2%)
    pallas_call x1, Pallas kernels, body(): pl.pallas_call(functools.partial(kernel, dims), out_shape=(jax.ShapeDtype...  30.5 us
    pallas_call x1, Pallas kernels, body(): pl.pallas_call(functools.partial(finish, tok, chans), out_shape=(jax.Shap...  1.35 us

profile of v6, /device:TPU:1, one launch (start us, length us, event | category | flops | bytes accessed | tf_op | source)
XLA Modules:
  0.0 32.5 jit_solution(6760600921531886684)
XLA Ops:
  0.6 30.5 %hyena.1 = (bf16[128,4096]{1,0:T(8,128)(2,1)S(1)}, f32[128,128]{1,0:T(8,128)S(1)}, f32[32,128]{1,0:T(8,128)S(1)}) custom-call(bf16[128,4096]{1,0:T(8,128)(2,1)} %q_hbm.1, bf16[128,4096]{1,0:T(8,128)(2,1)} %k_hbm.1, bf16[128,4096]{1,0:T(8,128)(2,1)} %v_hbm.1, bf16[128,4096]{1,0:T(8,128)(2,1)} %r_hbm.1, f32[3,7,4096]{2,1,0:T(8,128)} %sf_hbm.1, ...), custom_call_target="tpu_custom_call" | custom-call | tf_op jit(solution)/shard_map/hyena/pallas_call | solution.py:640
  31.2 1.4 %finish.1 = (bf16[128,4096]{1,0:T(8,128)(2,1)}, bf16[128,4096]{1,0:T(8,128)(2,1)}) custom-call(bf16[128,4096]{1,0:T(8,128)(2,1)S(1)} %get-tuple-element.5.stream_ref, f32[128,128]{1,0:T(8,128)S(1)} %get-tuple-element.6.scale_ref, f32[32,128]{1,0:T(8,128)S(1)} %get-tuple-element.7.gain_ref), custom_call_target="tpu_custom_call" | custom-call | tf_op jit(solution)/shard_map/finish/pallas_call | solution.py:683

commit v7 on v4

--- a/solution.py
+++ b/solution.py
@@ -22,7 +22,7 @@
     xq, xk, xv, zs, conv_std, qs_std,
     taps_t, rate_n, coef_n, dec_n, weights, dec8_n,
     keep_m, last_m, carry_m,
-    e_loc, e_buf, pre_buf, reach_buf, total_buf, plane_buf, inc_buf, sq_loc, sq_far,
+    e_loc, e_out, e_buf, pre_buf, reach_buf, total_buf, plane_buf, inc_out, inc_buf, sq_loc, sq_far,
     in_sem, param_sem, rim_send, rim_recv, edge_send, edge_recv, s1, r1, s2, r2, s3, r3, sq_send, sq_recv,
 ):
     shards, planes, tok, chans, modes, taps, segs = dims
@@ -83,7 +83,10 @@
         last = (zed - 1) * PLANE + PLANE - 1
         pl.semaphore_signal(barrier, inc=1, device_id=(last, core), device_id_type=MESH)
 
-    pl.semaphore_signal(barrier, inc=1, device_id=(before, core), device_id_type=MESH)
+    @pl.when(me > 0)
+    def _():
+        pl.semaphore_signal(barrier, inc=1, device_id=(before, core), device_id_type=MESH)
+
     pl.semaphore_signal(barrier, inc=1, device_id=(me, 1 - core), device_id_type=MESH)
 
     params[4].wait()
@@ -243,7 +246,7 @@
 
     crossing = ((spot + 1) // PLANE) * ((2 * planes - 3 - zed) // (planes - 1))
     crosses = crossing > 0
-    pl.semaphore_wait(barrier, PLANE - 1 + planes - 1 + 2 + PLANE * crossing)
+    pl.semaphore_wait(barrier, PLANE - 1 + planes - 1 + 1 + (2 * shards - 3 - me) // (shards - 1) + PLANE * crossing)
 
     def edge_copy(owner, slot, plane, kind):
         return pltpu.make_async_remote_copy(
@@ -274,17 +277,20 @@
 
     def round_1(other):
         return pltpu.make_async_remote_copy(
-            src_ref=at(e_loc, other * part, part), dst_ref=e_buf.at[spot],
+            src_ref=e_out.at[other], dst_ref=e_buf.at[spot],
             send_sem=s1.at[other], recv_sem=r1.at[spot],
             device_id=(zed * PLANE + other, core), device_id_type=MESH,
         )
 
     def arrival_1(other):
         return pltpu.make_async_remote_copy(
-            src_ref=at(e_loc, other * part, part), dst_ref=e_buf.at[other],
+            src_ref=e_out.at[other], dst_ref=e_buf.at[other],
             send_sem=s1.at[other], recv_sem=r1.at[other],
             device_id=(zed * PLANE + other, core), device_id_type=MESH,
         )
+
+    for other in range(PLANE):
+        e_out[other] = e_loc[other * part : (other + 1) * part, :].astype(jnp.bfloat16)
 
     @pl.loop(1, PLANE)
     def _(step):
@@ -298,10 +304,17 @@
         )
 
     rims = [rim_copy(0, k_hbm, rim_k), rim_copy(1, v_hbm, rim_v), rim_copy(2, q_hbm, rim_q)]
-    for copy in rims:
-        copy.start()
-
-    e_buf[spot] = at(e_loc, spot * part, part)[...]
+    @pl.when(me < shards - 1)
+    def _():
+        for copy in rims:
+            copy.start()
+
+    @pl.when(me == 0)
+    def _():
+        for rim in (rim_k, rim_v, rim_q):
+            rim[...] = jnp.zeros_like(rim)
+
+    e_buf[spot] = e_out[spot]
 
     begins = rows == 0
     for end in ends:
@@ -451,7 +464,7 @@
         pre_buf[other] = state
         reach_buf[other] = reach
         factor = span * open_here[other : other + 1]
-        state = factor * state + e_buf[other] + rest * e_first[other * part : (other + 1) * part, :]
+        state = factor * state + e_buf[other].astype(F32) + rest * e_first[other * part : (other + 1) * part, :]
         reach = factor * reach
     total_buf[...] = state
 
@@ -480,7 +493,7 @@
     state = lax.fori_loop(0, zed, plane_step, jnp.zeros_like(span))
     def round_3(other, slot):
         return pltpu.make_async_remote_copy(
-            src_ref=pre_buf.at[other], dst_ref=inc_buf.at[slot],
+            src_ref=inc_out.at[other], dst_ref=inc_buf.at[slot],
             send_sem=s3.at[other], recv_sem=r3.at[slot],
             device_id=(zed * PLANE + other, core), device_id_type=MESH,
         )
@@ -488,15 +501,18 @@
     @pl.loop(1, PLANE)
     def _(step):
         other = nth_of(PLANE - step)
-        pre_buf[other] = pre_buf[other] + reach_buf[other] * state
+        inc_out[other] = (pre_buf[other] + reach_buf[other] * state).astype(jnp.bfloat16)
         round_3(other, spot).start()
 
-    inc_buf[spot] = pre_buf[spot] + reach_buf[spot] * state
+    inc_buf[spot] = (pre_buf[spot] + reach_buf[spot] * state).astype(jnp.bfloat16)
 
     inner(groups - 1)
 
-    for copy in rims:
-        copy.wait_recv()
+    @pl.when(me > 0)
+    def _():
+        for copy in rims:
+            copy.wait_recv()
+
     relayout_rim(rim_k, xk)
     relayout_rim(rim_v, xv)
     relayout_rim(rim_q, xq)
@@ -523,7 +539,7 @@
     def tile_of(slot, local):
         t = slot * per + local
         whole = pl.ds(pl.multiple_of(t * modes, SUB), modes)
-        incoming = inc_buf[slot, local * modes : (local + 1) * modes, :]
+        incoming = inc_buf[slot].astype(F32)[local * modes : (local + 1) * modes]
         at_8 = dec8_n[whole, :] * carry_m[SUB - 1 : SUB, :] * incoming + head_n[whole, :]
         value, later, decay = [], [], []
         for m in range(modes):
@@ -566,8 +582,10 @@
     )
     swap.start()
 
-    for copy in rims:
-        copy.wait_send()
+    @pl.when(me < shards - 1)
+    def _():
+        for copy in rims:
+            copy.wait_send()
 
     @pl.loop(1, PLANE)
     def _(step):
@@ -661,8 +679,10 @@
             vmem((tiles * modes * SUB, LANES), F32), vmem((tiles * modes, LANES), F32),
             vmem((tok, LANES), F32), vmem((tok, LANES), F32), vmem((tok, LANES), F32),
             vmem((tiles * modes, LANES), F32),
-            vmem((PLANE, part, LANES), F32), vmem((PLANE, part, LANES), F32), vmem((PLANE, part, LANES), F32),
-            vmem((part, LANES), F32), vmem((planes, part, LANES), F32), vmem((PLANE, part, LANES), F32),
+            vmem((PLANE, part, LANES), bf16), vmem((PLANE, part, LANES), bf16),
+            vmem((PLANE, part, LANES), F32), vmem((PLANE, part, LANES), F32),
+            vmem((part, LANES), F32), vmem((planes, part, LANES), F32),
+            vmem((PLANE, part, LANES), bf16), vmem((PLANE, part, LANES), bf16),
             vmem((tok, LANES), F32), vmem((tok, LANES), F32),
             sem((4, groups)), sem((5,)), sem((3,)), sem((3,)), sem((2, PLANE)), sem((PLANE + 1,)),
             sem((PLANE,)), sem((PLANE,)), sem((planes,)), sem((planes,)), sem((PLANE,)), sem((PLANE,)),

time: 32.4 us -> 31.3 us (0.966)
  the two profiles are of different devices: /device:TPU:1 before, /device:TPU:33 now
where the time goes in v7:
time: 31.3 us; the launch traced here: 31.2 us
  Pallas kernels  30.6 us (98%)
  between operations  0.64 us (2%)
    pallas_call x1, Pallas kernels, body(): pl.pallas_call(functools.partial(kernel, dims), out_shape=(jax.ShapeDtype...  29.2 us
    pallas_call x1, Pallas kernels, body(): pl.pallas_call(functools.partial(finish, tok, chans), out_shape=(jax.Shap...  1.35 us

profile of v7, /device:TPU:33, one launch (start us, length us, event | category | flops | bytes accessed | tf_op | source)
XLA Modules:
  0.0 31.2 jit_solution(2343608803217897159)
XLA Ops:
  0.6 29.2 %hyena.1 = (bf16[128,4096]{1,0:T(8,128)(2,1)S(1)}, f32[128,128]{1,0:T(8,128)S(1)}, f32[32,128]{1,0:T(8,128)S(1)}) custom-call(bf16[128,4096]{1,0:T(8,128)(2,1)} %q_hbm.1, bf16[128,4096]{1,0:T(8,128)(2,1)} %k_hbm.1, bf16[128,4096]{1,0:T(8,128)(2,1)} %v_hbm.1, bf16[128,4096]{1,0:T(8,128)(2,1)} %r_hbm.1, f32[3,7,4096]{2,1,0:T(8,128)} %sf_hbm.1, ...), custom_call_target="tpu_custom_call" | custom-call | tf_op jit(solution)/shard_map/hyena/pallas_call | solution.py:653
  29.9 1.4 %finish.1 = (bf16[128,4096]{1,0:T(8,128)(2,1)}, bf16[128,4096]{1,0:T(8,128)(2,1)}) custom-call(bf16[128,4096]{1,0:T(8,128)(2,1)S(1)} %get-tuple-element.5.stream_ref, f32[128,128]{1,0:T(8,128)S(1)} %get-tuple-element.6.scale_ref, f32[32,128]{1,0:T(8,128)S(1)} %get-tuple-element.7.gain_ref), custom_call_target="tpu_custom_call" | custom-call | tf_op jit(solution)/shard_map/finish/pallas_call | solution.py:698

commit v8 on v7

--- a/solution.py
+++ b/solution.py
@@ -508,6 +508,22 @@
 
     inner(groups - 1)
 
+    for g in range(groups):
+        load(3, r_hbm, r_in, g).wait()
+
+    def add_residual(begin, end):
+        @pl.loop(0, tiles)
+        def _(t):
+            cols = pl.ds(pl.multiple_of(t * LANES, LANES), LANES)
+            for pair in range(begin, end):
+                x = r_in[pair * 2 * SUB : (pair + 1) * 2 * SUB, cols].astype(F32)
+                for half in range(2):
+                    here = pl.ds(pl.multiple_of(row_of(2 * pair + half, t), SUB), SUB)
+                    conv_std[here, :] = conv_std[here, :] + x[half * SUB : (half + 1) * SUB]
+
+    add_residual(1, pairs)
+    sq_loc[...] = jnp.zeros_like(sq_loc)
+
     @pl.when(me > 0)
     def _():
         for copy in rims:
@@ -521,19 +537,7 @@
     def _(g):
         head(g)
 
-    for g in range(groups):
-        load(3, r_hbm, r_in, g).wait()
-
-    @pl.loop(0, tiles)
-    def _(t):
-        cols = pl.ds(pl.multiple_of(t * LANES, LANES), LANES)
-        for pair in range(pairs):
-            x = r_in[pair * 2 * SUB : (pair + 1) * 2 * SUB, cols].astype(F32)
-            for half in range(2):
-                here = pl.ds(pl.multiple_of(row_of(2 * pair + half, t), SUB), SUB)
-                conv_std[here, :] = conv_std[here, :] + x[half * SUB : (half + 1) * SUB]
-
-    sq_loc[...] = jnp.zeros_like(sq_loc)
+    add_residual(0, 1)
 
 
     def tile_of(slot, local):

time: 31.3 us -> 31.2 us (level)
  the two profiles are of different devices: /device:TPU:33 before, /device:TPU:1 now
where the time goes in v8:
time: 31.2 us; the launch traced here: 30.6 us
  Pallas kernels  30 us (96%)
  between operations  0.64 us (2%)
    pallas_call x1, Pallas kernels, body(): pl.pallas_call(functools.partial(kernel, dims), out_shape=(jax.ShapeDtype...  28.6 us
    pallas_call x1, Pallas kernels, body(): pl.pallas_call(functools.partial(finish, tok, chans), out_shape=(jax.Shap...  1.35 us

profile of v8, /device:TPU:1, one launch (start us, length us, event | category | flops | bytes accessed | tf_op | source)
XLA Modules:
  0.0 30.6 jit_solution(3545293794031944176)
XLA Ops:
  0.6 28.6 %hyena.1 = (bf16[128,4096]{1,0:T(8,128)(2,1)S(1)}, f32[128,128]{1,0:T(8,128)S(1)}, f32[32,128]{1,0:T(8,128)S(1)}) custom-call(bf16[128,4096]{1,0:T(8,128)(2,1)} %q_hbm.1, bf16[128,4096]{1,0:T(8,128)(2,1)} %k_hbm.1, bf16[128,4096]{1,0:T(8,128)(2,1)} %v_hbm.1, bf16[128,4096]{1,0:T(8,128)(2,1)} %r_hbm.1, f32[3,7,4096]{2,1,0:T(8,128)} %sf_hbm.1, ...), custom_call_target="tpu_custom_call" | custom-call | tf_op jit(solution)/shard_map/hyena/pallas_call | solution.py:657
  29.3 1.4 %finish.1 = (bf16[128,4096]{1,0:T(8,128)(2,1)}, bf16[128,4096]{1,0:T(8,128)(2,1)}) custom-call(bf16[128,4096]{1,0:T(8,128)(2,1)S(1)} %get-tuple-element.5.stream_ref, f32[128,128]{1,0:T(8,128)S(1)} %get-tuple-element.6.scale_ref, f32[32,128]{1,0:T(8,128)S(1)} %get-tuple-element.7.gain_ref), custom_call_target="tpu_custom_call" | custom-call | tf_op jit(solution)/shard_map/finish/pallas_call | solution.py:702

commit v9 on v8

--- a/solution.py
+++ b/solution.py
@@ -524,14 +524,25 @@
     add_residual(1, pairs)
     sq_loc[...] = jnp.zeros_like(sq_loc)
 
-    @pl.when(me > 0)
-    def _():
-        for copy in rims:
-            copy.wait_recv()
-
-    relayout_rim(rim_k, xk)
-    relayout_rim(rim_v, xv)
-    relayout_rim(rim_q, xq)
+    @pl.loop(1, PLANE)
+    def _(step):
+        other = lax.rem(spot + step, PLANE)
+        round_1(other).wait_send()
+        edge_copy(other, spot, zed, 0).wait_send()
+
+    @pl.when(crosses)
+    def _():
+        @pl.loop(0, PLANE)
+        def _(owner):
+            edge_copy(owner, PLANE, zed + 1, 1).wait_send()
+
+    @pl.loop(zed + 1, planes)
+    def _(there):
+        round_2(there, zed).wait_send()
+
+    for copy, rim, dst in zip(rims, (rim_k, rim_v, rim_q), (xk, xv, xq)):
+        pl.when(me > 0)(copy.wait_recv)
+        relayout_rim(rim, dst)
 
     @pl.loop(0, groups)
     def _(g):
@@ -594,19 +605,7 @@
     @pl.loop(1, PLANE)
     def _(step):
         other = lax.rem(spot + step, PLANE)
-        round_1(other).wait_send()
         round_3(other, spot).wait_send()
-        edge_copy(other, spot, zed, 0).wait_send()
-
-    @pl.when(crosses)
-    def _():
-        @pl.loop(0, PLANE)
-        def _(owner):
-            edge_copy(owner, PLANE, zed + 1, 1).wait_send()
-
-    @pl.loop(zed + 1, planes)
-    def _(there):
-        round_2(there, zed).wait_send()
 
     swap.wait()
     total = jnp.sum(sq_loc[...] + sq_far[...], axis=1, keepdims=True)

time: 31.2 us -> 31.2 us (level)
  no operation moved by 1% of the time
where the time goes in v9:
time: 31.2 us; the launch traced here: 30.9 us
  Pallas kernels  30.3 us (97%)
  between operations  0.64 us (2%)
    pallas_call x1, Pallas kernels, body(): pl.pallas_call(functools.partial(kernel, dims), out_shape=(jax.ShapeDtype...  28.9 us
    pallas_call x1, Pallas kernels, body(): pl.pallas_call(functools.partial(finish, tok, chans), out_shape=(jax.Shap...  1.35 us

profile of v9, /device:TPU:1, one launch (start us, length us, event | category | flops | bytes accessed | tf_op | source)
XLA Modules:
  0.0 30.9 jit_solution(5809285438416866743)
XLA Ops:
  0.6 28.9 %hyena.1 = (bf16[128,4096]{1,0:T(8,128)(2,1)S(1)}, f32[128,128]{1,0:T(8,128)S(1)}, f32[32,128]{1,0:T(8,128)S(1)}) custom-call(bf16[128,4096]{1,0:T(8,128)(2,1)} %q_hbm.1, bf16[128,4096]{1,0:T(8,128)(2,1)} %k_hbm.1, bf16[128,4096]{1,0:T(8,128)(2,1)} %v_hbm.1, bf16[128,4096]{1,0:T(8,128)(2,1)} %r_hbm.1, f32[3,7,4096]{2,1,0:T(8,128)} %sf_hbm.1, ...), custom_call_target="tpu_custom_call" | custom-call | tf_op jit(solution)/shard_map/hyena/pallas_call | solution.py:656
  29.5 1.4 %finish.1 = (bf16[128,4096]{1,0:T(8,128)(2,1)}, bf16[128,4096]{1,0:T(8,128)(2,1)}) custom-call(bf16[128,4096]{1,0:T(8,128)(2,1)S(1)} %get-tuple-element.5.stream_ref, f32[128,128]{1,0:T(8,128)S(1)} %get-tuple-element.6.scale_ref, f32[32,128]{1,0:T(8,128)S(1)} %get-tuple-element.7.gain_ref), custom_call_target="tpu_custom_call" | custom-call | tf_op jit(solution)/shard_map/finish/pallas_call | solution.py:701

commit v10 on v8

--- a/solution.py
+++ b/solution.py
@@ -615,13 +615,14 @@
 
 
 def finish(tok, chans, stream_ref, scale_ref, gain_ref, stream_hbm, normed_hbm, normed, sem):
-    wide = SUB * LANES
+    each = SUB // 2
+    wide = each * LANES
     groups = chans // wide
     copies = [pltpu.make_async_copy(stream_ref, stream_hbm, sem.at[groups])]
     copies[0].start()
     scales = [scale_ref[pair * 2 * SUB : (pair + 1) * 2 * SUB, :] for pair in range(tok // (2 * SUB))]
     for g in range(groups):
-        @pl.loop(g * SUB, (g + 1) * SUB)
+        @pl.loop(g * each, (g + 1) * each)
         def _(t):
             cols = pl.ds(pl.multiple_of(t * LANES, LANES), LANES)
             gain = gain_ref[pl.ds(t, 1), :]
@@ -704,7 +705,7 @@
         out_shape=(jax.ShapeDtypeStruct((tok, chans), bf16),) * 2,
         in_specs=[pl.BlockSpec(memory_space=vmem)] * 3,
         out_specs=(hbm_spec,) * 2,
-        scratch_shapes=[vmem((tok, chans), bf16), sem((chans // (SUB * LANES) + 1,))],
+        scratch_shapes=[vmem((tok, chans), bf16), sem((2 * chans // (SUB * LANES) + 1,))],
         compiler_params=pltpu.CompilerParams(vmem_limit_bytes=16 * 1024 * 1024),
         name="finish",
     )(stream, scale, gain)

time: 31.2 us -> 31.2 us (level)
  no operation moved by 1% of the time
where the time goes in v10:
time: 31.2 us; the launch traced here: 30.6 us
  Pallas kernels  30 us (96%)
  between operations  0.64 us (2%)
    pallas_call x1, Pallas kernels, body(): pl.pallas_call(functools.partial(kernel, dims), out_shape=(jax.ShapeDtype...  28.6 us
    pallas_call x1, Pallas kernels, body(): pl.pallas_call(functools.partial(finish, tok, chans), out_shape=(jax.Shap...  1.38 us

profile of v10, /device:TPU:1, one launch (start us, length us, event | category | flops | bytes accessed | tf_op | source)
XLA Modules:
  0.0 30.6 jit_solution(13390086041384672212)
XLA Ops:
  0.6 28.6 %hyena.1 = (bf16[128,4096]{1,0:T(8,128)(2,1)S(1)}, f32[128,128]{1,0:T(8,128)S(1)}, f32[32,128]{1,0:T(8,128)S(1)}) custom-call(bf16[128,4096]{1,0:T(8,128)(2,1)} %q_hbm.1, bf16[128,4096]{1,0:T(8,128)(2,1)} %k_hbm.1, bf16[128,4096]{1,0:T(8,128)(2,1)} %v_hbm.1, bf16[128,4096]{1,0:T(8,128)(2,1)} %r_hbm.1, f32[3,7,4096]{2,1,0:T(8,128)} %sf_hbm.1, ...), custom_call_target="tpu_custom_call" | custom-call | tf_op jit(solution)/shard_map/hyena/pallas_call | solution.py:658
  29.3 1.4 %finish.1 = (bf16[128,4096]{1,0:T(8,128)(2,1)}, bf16[128,4096]{1,0:T(8,128)(2,1)}) custom-call(bf16[128,4096]{1,0:T(8,128)(2,1)S(1)} %get-tuple-element.5.stream_ref, f32[128,128]{1,0:T(8,128)S(1)} %get-tuple-element.6.scale_ref, f32[32,128]{1,0:T(8,128)S(1)} %get-tuple-element.7.gain_ref), custom_call_target="tpu_custom_call" | custom-call | tf_op jit(solution)/shard_map/finish/pallas_call | solution.py:703
